TPU v7x, 512 devices: a whole 4x4x16 slice. The times are simulated.
512 devices in a mesh: rowg: 16 (over y_hi, x, core), colg: 32 (over y_lo, z).
Axes of the slice: x: 4, y: 4 (y_hi: 2, y_lo: 2; y = y_hi * 2 + y_lo), z: 16, core: 2. Of those that a mesh axis runs over, the one named last changes fastest.
Arguments:
- pair_rows: int32 [8192, 32768], P('rowg', 'colg'), may hold values from 0 to 240
- reducers: int32 [2, 1024, 32768], P(None, 'rowg', 'colg'), may hold values from 0 to 240
- pivots: int32 [2, 1024], replicated, may hold values from 0 to 32767, as said below
- counts: int32 [16], replicated, may hold values from 0 to 512, as said below
Outputs:
- reduced: int32 [4096, 32768], P('rowg', 'colg')
Inputs may be any that keep to these rules, and one draw needn't show every extreme that they name: `pivots`: the 2048 pivot columns are all different; column 0 and column 32767 are among them. `counts`: owners 2i and 2i + 1 together hold 512 live rows; some owner has exactly 512 live rows and its partner none; owner 16 - 2 holds more than 256 live rows.
All inputs are finite; a program needn't handle non-finite values.
Results may differ from a plain program's by a relative error of at most 0.000001.
Values may be sent and summed in bfloat16 or wider, within the bound.
No kernel may reach another device: no remote copies, remote signals or barrier semaphores. Data moves between devices by JAX's collectives and lax.ppermute only.
A program may use at most 64 MiB of HBM per device.

v0:
```python
import jax
import jax.numpy as jnp
from jax import lax
from jax.sharding import PartitionSpec as P

PANELS = 2
LIVE_DEV = 256


modulus = 241.0
half_modulus = 120.0


def partner_2(value, axis, stride):
    return lax.ppermute(value, axis, [(i, i ^ 1 << stride) for i in range(lax.axis_size(axis))])


def centered(values):
    return values - modulus * (values > half_modulus).astype(values.dtype)


def pick_value(table, position):
    marks = lax.iota(jnp.int32, table.shape[0]) == position
    return jnp.sum(jnp.where(marks, table, jnp.zeros_like(table)))


def place_rows(source, my_start, my_count, target, live_dev):
    slot_count = source.shape[0]
    rank_ids = target * live_dev + lax.iota(jnp.int32, live_dev)
    offsets = rank_ids - my_start
    valid = (offsets >= 0) & (offsets < my_count)
    picked = jnp.take(source, jnp.clip(offsets, 0, slot_count - 1), axis=0)
    return jnp.where(valid[:, None], picked, jnp.zeros_like(picked))


def normalize_block(block, pivot_cols, all_pivots, row_index, col_start):
    block_rows = block.shape[0]
    col_width = block.shape[1]
    columns = col_start + lax.iota(jnp.int32, col_width)
    is_pivot = jnp.any(columns[:, None] == all_pivots[None, :], axis=1)
    own_cols = lax.dynamic_slice_in_dim(pivot_cols, row_index * block_rows, block_rows)
    own_pivot = columns[None, :] == own_cols[:, None]
    entries = centered(block.astype(jnp.float32))
    ones = jnp.ones_like(entries)
    zeros = jnp.zeros_like(entries)
    kept = jnp.where(is_pivot[None, :], jnp.where(own_pivot, ones, zeros), entries)
    return kept.astype(jnp.bfloat16)


def local_columns(matrix_rows, pivot_cols, col_start):
    col_width = matrix_rows.shape[1]
    offsets = pivot_cols - col_start
    inside = (offsets >= 0) & (offsets < col_width)
    taken = jnp.take(matrix_rows, jnp.clip(offsets, 0, col_width - 1), axis=1)
    return jnp.where(inside[None, :], taken, jnp.zeros_like(taken)).astype(jnp.bfloat16)


def folded_product(factors, normed):
    return jnp.dot(
        factors,
        lax.all_gather(normed, "rowg", axis=0, tiled=True),
        preferred_element_type=jnp.float32,
    )


def shards(pair_rows, reducers, pivots, counts):
    row_index = lax.axis_index("rowg")
    col_index = lax.axis_index("colg")
    col_width = pair_rows.shape[1]
    col_start = col_index * col_width
    live_dev = LIVE_DEV
    partner = row_index + 1 - 2 * (row_index % 2)
    ends = jnp.cumsum(counts)
    starts = ends - counts
    my_start = pick_value(starts, row_index)
    my_count = pick_value(counts, row_index)
    all_pivots = pivots.reshape(-1)
    normed_list = [
        normalize_block(reducers[panel], pivots[panel], all_pivots, row_index, col_start)
        for panel in range(PANELS)
    ]
    matrix_rows = pair_rows.astype(jnp.float32)
    for panel in range(PANELS):
        taken = local_columns(matrix_rows, pivots[panel], col_start)
        summed = lax.psum(taken, "colg").astype(jnp.float32)
        factors = centered(summed).astype(jnp.bfloat16)
        product = folded_product(factors, normed_list[panel])
        matrix_rows = jnp.mod(matrix_rows - product, modulus)
    source = matrix_rows.astype(jnp.bfloat16)
    kept = place_rows(source, my_start, my_count, row_index, live_dev)
    outgoing = place_rows(source, my_start, my_count, partner, live_dev)
    incoming = partner_2(outgoing, "rowg", 0)
    result = kept.astype(jnp.float32) + incoming.astype(jnp.float32)
    return result.astype(jnp.int32)


def solution(mesh):
    return jax.shard_map(
        shards,
        mesh=mesh,
        in_specs=(P("rowg", "colg"), P(None, "rowg", "colg"), P(), P()),
        out_specs=P("rowg", "colg"),
        check_vma=False,
    )
```

profile of v0, /device:TPU:1, one launch (start us, length us, event | category | flops | bytes accessed | tf_op | source)
XLA Modules:
  0.0 569.9 jit_solution(17326288771651892807)
XLA Ops:
  7.4 0.8 subtract_clamp_fusion
  8.2 0.8 and_reduce_fusion
  9.0 1.8 convert_element_type.55
  10.9 0.5 copy.16
  11.4 4.0 gather_fusion
  15.9 1.2 fusion.4
  17.4 1.2 compare_reduce_fusion
  18.5 1.9 fusion.14
  21.1 240.5 %all-reduce.3.cloned.1.call-done = bf16[512,1024]{1,0:T(8,128)(2,1)} async-done(((bf16[512,1024]{1,0:T(8,128)(2,1)}), bf16[512,1024]{1,0:T(8,128)(2,1)}) %all-reduce.3.cloned.1.call-update) | async-done | bytes 1048592 | tf_op jit(solution)/shard_map/psum | solution.py:85
  261.6 5.4 add_select_fusion.1
  267.0 1.8 copy.18
  268.8 4.0 gather_fusion.1
  273.3 1.2 fusion.3
  274.8 0.7 fusion.20
  275.5 0.6 compare_select_fusion.2
  276.2 1.3 compare_and_fusion.2
  277.5 250.6 %all-reduce.5.cloned.1.call-done = bf16[512,1024]{1,0:T(8,128)(2,1)} async-done(((bf16[512,1024]{1,0:T(8,128)(2,1)}), bf16[512,1024]{1,0:T(8,128)(2,1)}) %all-reduce.5.cloned.1.call-update) | async-done | bytes 1048592 | tf_op jit(solution)/shard_map/psum | solution.py:85
  528.1 4.1 fusion.2
  532.2 1.2 gather_fusion.3
  533.5 24.6 %collective-permute-start = (bf16[256,1024]{1,0:T(8,128)(2,1)S(1)}, bf16[256,1024]{1,0:T(8,128)(2,1)S(1)}, u32[]{:S(2)}, u32[]{:S(2)}) collective-permute-start(bf16[256,1024]{1,0:T(8,128)(2,1)S(1)} %select_select_fusion), channel_id=1, source_target_pairs={{0,32},{32,0},{64,96},{96,64},{128,160},{160,128},{192,224},{224,1... | collective-permute-start | bytes 1572872 | tf_op jit(solution)/shard_map/ppermute | solution.py:15
  558.1 0.6 compare_select_fusion.3
  558.7 1.3 compare_and_fusion.3
  560.0 1.2 gather_fusion.2
  561.2 1.3 add_convert_fusion
  (34 shorter events, 2.3 us)
Async XLA Ops:
  7.4 254.2 %all-reduce.3.cloned.1.call-start = ((), (), s32[]{:S(2)}) async-start(), calls=%async_computation | async-start | bytes 2097152 | tf_op jit(solution)/shard_map/psum | solution.py:85
  15.9 1.3 copy-start.2
  15.9 245.7 %copy-start = (s32[512,1024]{1,0:T(8,128)S(1)}, s32[512,1024]{1,0:T(8,128)}, u32[]{:S(2)}) copy-start(s32[512,1024]{1,0:T(8,128)} %param.8) | copy-start | bytes 6291460
  17.2 244.4 %all-gather.3.cloned.1.call-start = ((), (), s32[]{:S(2)}) async-start(), calls=%async_computation.1 | async-start | bytes 2228224 | tf_op jit(solution)/shard_map/all_gather | solution.py:61
  20.4 257.1 %all-gather.5.cloned.1.call-start = ((), (), s32[]{:S(2)}) async-start(), calls=%async_computation.3 | async-start | bytes 2228224 | tf_op jit(solution)/shard_map/all_gather | solution.py:61
  21.0 507.1 %all-reduce.5.cloned.1.call-start = ((), (), s32[]{:S(2)}) async-start(), calls=%async_computation.2 | async-start | bytes 2097152 | tf_op jit(solution)/shard_map/psum | solution.py:85
  273.3 1.3 copy-start.3
  273.3 254.8 %copy-start.1 = (f32[512,1024]{1,0:T(8,128)S(1)}, f32[512,1024]{1,0:T(8,128)}, u32[]{:S(2)}) copy-start(f32[512,1024]{1,0:T(8,128)} %add_select_fusion.1) | copy-start | bytes 6291460
  533.5 27.7 %collective-permute-start = (bf16[256,1024]{1,0:T(8,128)(2,1)S(1)}, bf16[256,1024]{1,0:T(8,128)(2,1)S(1)}, u32[]{:S(2)}, u32[]{:S(2)}) collective-permute-start(bf16[256,1024]{1,0:T(8,128)(2,1)S(1)} %select_select_fusion), channel_id=1, source_target_pairs={{0,32},{32,0},{64,96},{96,64},{128,160},{160,128},{192,224},{224,1... | collective-permute-start | bytes 1572872 | tf_op jit(solution)/shard_map/ppermute | solution.py:15
Sparse Core Ops, SparseCore 0:
  17.3 244.2 all-reduce.2
  274.7 253.3 all-reduce.4
Sparse Core Ops, SparseCore 1:
  21.0 69.8 all-gather.2
  94.1 62.1 all-gather.4
where the time goes:
time: 570 us
  waiting for transfers between devices  492 us (86%)
  starting transfers between devices  24.7 us (4%)
  other arithmetic  15.1 us (3%)
  between operations  15.1 us (3%)
  local copies, waits for them, and re-layouts  13.8 us (2%)
  matrix products  9.46 us (2%)
    psum x2, waiting for transfers between devices, shards(): summed = lax.psum(taken, 'colg').astype(jnp.float32)  491 us
    ppermute x1, starting transfers between devices, partner_2(): lax.ppermute(value, axis, [(i, i ^ 1 << stride) for i in range(lax.axis_s...  24.6 us
  transfers between devices with their start and end apart: 5, of which 2 were waited for; matrix products, arithmetic and copies ran while one was open for 4% of the time, Pallas kernels for 0%

commit v1 on v0

v1 whole, which is shorter than its diff:
```python
import jax
import jax.numpy as jnp
from jax import lax
from jax.sharding import Mesh, PartitionSpec as P

PANELS = 2
LIVE_DEV = 256
CAP = 96

ROW = ("yh", "x", "core")
COL = ("yl", "z")

modulus = 241.0
half_modulus = 120.0


def centered(values):
    return values - modulus * (values > half_modulus).astype(values.dtype)


def pick_value(table, position):
    marks = lax.iota(jnp.int32, table.shape[0]) == position
    return jnp.sum(jnp.where(marks, table, jnp.zeros_like(table)))


def swap(value, axis):
    return lax.ppermute(value, axis, [(0, 1), (1, 0)])


def take_window(source, start, rows):
    index = start + lax.iota(jnp.int32, rows)
    return jnp.take(source, jnp.clip(index, 0, source.shape[0] - 1), axis=0)


def compact_rows(pair_rows, counts):
    row_index = lax.axis_index(ROW)
    second = lax.axis_index("core")
    first_count = pick_value(counts, row_index - second)
    slots = pair_rows.astype(jnp.float32).astype(jnp.bfloat16)
    keep_start = second * (LIVE_DEV - first_count)
    send_start = jnp.where(second == 0, LIVE_DEV, -first_count)
    kept = take_window(slots, keep_start, LIVE_DEV)
    incoming = swap(take_window(slots, send_start, LIVE_DEV), "core")
    place = lax.iota(jnp.int32, LIVE_DEV)
    mine = jnp.where(second == 0, place < first_count, place >= first_count - LIVE_DEV)
    return jnp.where(mine[:, None], kept, incoming)


def normalize_block(block, own_cols, all_pivots, col_start):
    columns = col_start + lax.iota(jnp.int32, block.shape[1])
    is_pivot = jnp.any(columns[:, None] == all_pivots[None, :], axis=1)
    own_pivot = columns[None, :] == own_cols[:, None]
    entries = centered(block.astype(jnp.float32))
    ones = jnp.ones_like(entries)
    zeros = jnp.zeros_like(entries)
    kept = jnp.where(is_pivot[None, :], jnp.where(own_pivot, ones, zeros), entries)
    return kept.astype(jnp.bfloat16)


def shards(pair_rows, reducers, pivots, counts):
    row_index = lax.axis_index(ROW)
    col_index = lax.axis_index(COL)
    lower = lax.axis_index("yl")
    col_width = pair_rows.shape[1]
    col_start = col_index * col_width
    rows_dev = reducers.shape[1]
    order = pivots.reshape(PANELS, -1, rows_dev).transpose(1, 0, 2).reshape(-1)
    total = order.shape[0]
    own_cols = lax.dynamic_slice_in_dim(order, row_index * PANELS * rows_dev, PANELS * rows_dev)
    normed = normalize_block(reducers.reshape(PANELS * rows_dev, col_width), own_cols, order, col_start)
    panel = lax.all_gather(normed, ROW, axis=0, tiled=True)

    live = compact_rows(pair_rows, counts)

    owner = order // col_width
    ids = lax.iota(jnp.int32, total)
    same = owner[:, None] == owner[None, :]
    rank = jnp.sum((same & (ids[None, :] < ids[:, None])).astype(jnp.int32), axis=1)
    rounds = jnp.max(rank) // CAP + 1
    z_size = lax.axis_size("z")
    slot = (owner % z_size) * (2 * CAP) + (owner // z_size) * CAP

    def fetch(step):
        base = step * CAP
        want = base + lax.iota(jnp.int32, CAP)
        hit = (owner == col_index)[None, :] & (rank[None, :] == want[:, None])
        local = jnp.sum(jnp.where(hit, order[None, :] - col_start + 1, 0), axis=1) - 1
        choose = (local[:, None] == lax.iota(jnp.int32, col_width)[None, :]).astype(jnp.bfloat16)
        mine = lax.dot_general(choose, live, (((1,), (1,)), ((), ())), preferred_element_type=jnp.float32)
        mine = centered(mine).astype(jnp.bfloat16)
        theirs = swap(mine, "yl")
        both = jnp.where(lower == 0, jnp.stack([mine, theirs]), jnp.stack([theirs, mine]))
        spread = lax.all_gather(both.reshape(2 * CAP, LIVE_DEV), "z", axis=0, tiled=True)
        inside = (rank >= base) & (rank < base + CAP)
        got = jnp.take(spread, jnp.where(inside, slot + rank - base, 0), axis=0)
        return jnp.where(inside[:, None], got, jnp.zeros_like(got))

    half = total // 2

    def reduce_by(result, factors):
        for part in range(2):
            product = lax.dot_general(
                factors[part * half:(part + 1) * half],
                panel[part * half:(part + 1) * half],
                (((0,), (0,)), ((), ())),
                preferred_element_type=jnp.float32,
            )
            result = jnp.mod(result - product, modulus)
        return result

    first = reduce_by(live.astype(jnp.float32), fetch(0)).astype(jnp.int32)
    _, result = lax.while_loop(
        lambda state: state[0] < rounds,
        lambda state: (
            state[0] + 1,
            reduce_by(state[1].astype(jnp.float32), fetch(state[0])).astype(jnp.int32),
        ),
        (jnp.int32(1), first),
    )
    return result


def solution(mesh):
    fine = Mesh(mesh.devices.reshape(2, 4, 2, 2, 16), (*ROW, *COL))
    return jax.shard_map(
        shards,
        mesh=fine,
        in_specs=(P(ROW, COL), P(None, ROW, COL), P(), P()),
        out_specs=P(ROW, COL),
        check_vma=False,
    )
```

time: 570 us -> 194 us (0.34)
  waiting for transfers between devices: 492 us -> 132 us
  starting transfers between devices: 24.7 us -> 10.8 us
    psum x2 -> x0, waiting for transfers between devices: 491 us -> none  [shards(): summed = lax.psum(taken, 'colg').astype(jnp.float32)]
    all_gather x2, waiting for transfers between devices: 0.03 us -> 129 us  [the longest x1 72.3 us: shards(): panel = lax.all_gather(normed, ROW, axis=0, tiled=True)]
    ppermute x1 -> x2, starting transfers between devices: 24.6 us -> 10.8 us  [swap(): return lax.ppermute(value, axis, [(0, 1), (1, 0)])]
  transfers between devices with their start and end apart: 5 -> 4, of which waited for: 2 -> 3; matrix products, arithmetic and copies ran while one was open for 4% -> 10% of each run, Pallas kernels for 0% -> 0%
where the time goes in v1:
time: 194 us
  waiting for transfers between devices  132 us (68%)
  between operations  17.4 us (9%)
  other arithmetic  14.9 us (8%)
  local copies, waits for them, and re-layouts  12.7 us (7%)
  starting transfers between devices  10.8 us (6%)
  matrix products  5.73 us (3%)
    all_gather x1, waiting for transfers between devices, shards(): panel = lax.all_gather(normed, ROW, axis=0, tiled=True)  72.3 us
    all_gather x1, waiting for transfers between devices, fetch(): lax.all_gather(both.reshape(2 * CAP, LIVE_DEV), 'z', axis=0, tiled=True)  56.7 us
    ppermute x2, starting transfers between devices, swap(): return lax.ppermute(value, axis, [(0, 1), (1, 0)])  10.8 us
    gather x1, local copies, waits for them, and re-layouts, fetch(): got = jnp.take(spread, jnp.where(inside, slot + rank - base, 0), axis=0)  8.24 us
    dot_general x2, matrix products, reduce_by(): lax.dot_general(factors[part * half:(part + 1) * half], panel[part * half...  5.42 us
    reduce_sum x1, other arithmetic, shards(): jnp.sum((same & (ids[None, :] < ids[:, None])).astype(jnp.int32), axis=1)  4.48 us
  transfers between devices with their start and end apart: 4, of which 3 were waited for; matrix products, arithmetic and copies ran while one was open for 10% of the time, Pallas kernels for 0%

profile of v1, /device:TPU:1, one launch (start us, length us, event | category | flops | bytes accessed | tf_op | source)
XLA Modules:
  0.0 193.9 jit_solution(13259388793298008587)
XLA Ops:
  6.5 1.3 fusion.55
  8.5 1.8 convert_convert_fusion
  10.4 1.2 gather_fusion.3
  11.7 8.9 %collective-permute-start.1 = (bf16[256,1024]{1,0:T(8,128)(2,1)S(1)}, bf16[256,1024]{1,0:T(8,128)(2,1)S(1)}, u32[]{:S(2)}, u32[]{:S(2)}) collective-permute-start(bf16[256,1024]{1,0:T(8,128)(2,1)S(1)} %broadcast_select_fusion), channel_id=1, source_target_pairs={{0,32},{32,0},{1,33},{33,1},{2,34},{34,2},{3,35},{35,3},{4,36},{36... | collective-permute-start | bytes 1572872 | tf_op jit(solution)/shard_map/ppermute | solution.py:27
  21.5 4.5 %convert_reduce_fusion = s32[2048]{0:T(1024)S(1)} fusion(s32[2048]{0:T(1024)S(1)} %get-tuple-element.336), kind=kLoop, calls=%fused_computation.34 | loop fusion | flops 20969472 | bytes 16384 | tf_op jit(solution)/shard_map/reduce_sum | solution.py:78
  26.6 1.2 gather_fusion.2
  27.8 0.7 compare_and_fusion.5
  28.4 0.3 select_reduce_fusion.1
  28.7 0.8 copy-done.3
  29.5 1.2 select_select_fusion.2
  30.7 0.3 subtract_convert_fusion.1
  31.0 1.9 collective-permute-start.2
  33.0 3.2 %collective-permute-done.2 = bf16[96,256]{1,0:T(8,128)(2,1)S(1)} collective-permute-done((bf16[96,256]{1,0:T(8,128)(2,1)S(1)}, bf16[96,256]{1,0:T(8,128)(2,1)S(1)}, u32[]{:S(2)}, u32[]{:S(2)}) %collective-permute-start.2) | collective-permute-done | bytes 49184 | tf_op jit(solution)/shard_map/ppermute | solution.py:27
  36.2 0.6 maximum_select_fusion.1
  37.0 1.2 compare_reduce_fusion
  38.2 0.8 fusion.39
  39.1 0.7 reduce_max.9
  41.8 56.7 %all-gather.4.cloned.1.call-done = bf16[3072,256]{1,0:T(8,128)(2,1)} async-done(((bf16[192,256]{1,0:T(8,128)(2,1)}), bf16[3072,256]{1,0:T(8,128)(2,1)}) %all-gather.4.cloned.1.call-update) | async-done | bytes 1572880 | tf_op jit(solution)/shard_map/all_gather | solution.py:93
  98.6 8.2 %gather_fusion.1 = bf16[2048,256]{1,0:T(8,128)(2,1)S(1)} fusion(bf16[3072,256]{1,0:T(8,128)(2,1)} %all-gather.4.cloned.1.call-done, s32[2048]{0:T(1024)S(1)} %broadcast_clamp_fusion.1), kind=kCustom, calls=%fused_computation.3 | custom fusion | bytes 2105344 | tf_op jit(solution)/shard_map/jit(_take)/gather | solution.py:95
  106.8 1.5 select_select_fusion.1
  108.3 72.3 %all-gather.6.cloned.1.call-done = bf16[2048,1024]{1,0:T(8,128)(2,1)} async-done(((bf16[128,1024]{1,0:T(8,128)(2,1)}), bf16[2048,1024]{1,0:T(8,128)(2,1)}) %all-gather.6.cloned.1.call-update) | async-done | bytes 4194320 | tf_op jit(solution)/shard_map/all_gather | solution.py:71
  180.6 2.3 %fusion.26 = f32[256,1024]{1,0:T(8,128)S(1)} fusion(bf16[2048,1024]{1,0:T(8,128)(2,1)} %all-gather.6.cloned.1.call-done, bf16[2048,256]{1,0:T(8,128)(2,1)S(1)} %select_select_fusion.1), kind=kOutput, calls=%fused_computation.40 | convolution fusion | flops 536870912 | bytes 3670016 | tf_op jit(solution)/shard_map/dot_general | solution.py:102
  183.0 3.1 %fusion.30 = s32[256,1024]{1,0:T(8,128)S(1)} fusion(f32[256,1024]{1,0:T(8,128)S(1)} %fusion.26, bf16[256,1024]{1,0:T(8,128)(2,1)S(1)} %select_select_fusion.2, bf16[2048,1024]{1,0:T(8,128)(2,1)} %all-gather.6.cloned.1.call-done, bf16[2048,256]{1,0:T(8,128)(2,1)S(1)} %select_select_fusion.1), kind=kOutput, calls=%fused_computation.47 | convolution fusion | flops 541065216 | bytes 5242880 | tf_op jit(solution)/shard_map/dot_general | solution.py:102
  186.1 1.0 copy-done.1
  (30 shorter events, 0.8 us)
Async XLA Ops:
  6.5 92.0 %all-gather.4.cloned.1.call-start = ((), (), s32[]{:S(2)}) async-start(), calls=%async_computation | async-start | bytes 1671168 | tf_op jit(solution)/shard_map/all_gather | solution.py:93
  8.5 12.7 %copy-start.4 = (s32[2,1024]{1,0:T(2,128)S(1)}, s32[2,1024]{1,0:T(2,128)}, u32[]{:S(2)}) copy-start(s32[2,1024]{1,0:T(2,128)} %param.10) | copy-start | bytes 24580
  11.6 26.6 %copy-start.2 = (s32[2,64,1024]{2,1,0:T(8,128)S(1)}, s32[2,64,1024]{2,1,0:T(8,128)}, u32[]{:S(2)}) copy-start(s32[2,64,1024]{2,1,0:T(8,128)} %param.9) | copy-start | bytes 1572868
  11.7 17.0 %collective-permute-start.1 = (bf16[256,1024]{1,0:T(8,128)(2,1)S(1)}, bf16[256,1024]{1,0:T(8,128)(2,1)S(1)}, u32[]{:S(2)}, u32[]{:S(2)}) collective-permute-start(bf16[256,1024]{1,0:T(8,128)(2,1)S(1)} %broadcast_select_fusion), channel_id=1, source_target_pairs={{0,32},{32,0},{1,33},{33,1},{2,34},{34,2},{3,35},{35,3},{4,36},{36... | collective-permute-start | bytes 1572872 | tf_op jit(solution)/shard_map/ppermute | solution.py:27
  28.7 0.8 copy-start.3
  31.0 5.2 %collective-permute-start.2 = (bf16[96,256]{1,0:T(8,128)(2,1)S(1)}, bf16[96,256]{1,0:T(8,128)(2,1)S(1)}, u32[]{:S(2)}, u32[]{:S(2)}) collective-permute-start(bf16[96,256]{1,0:T(8,128)(2,1)S(1)} %subtract_convert_fusion.1), channel_id=1, source_target_pairs={{0,16},{16,0},{1,17},{17,1},{2,18},{18,2},{3,19},{19,3},{4,20},{20... | collective-permute-start | bytes 147464 | tf_op jit(solution)/shard_map/ppermute | solution.py:27
  36.9 143.8 %all-gather.6.cloned.1.call-start = ((), (), s32[]{:S(2)}) async-start(), calls=%async_computation.1 | async-start | bytes 4456448 | tf_op jit(solution)/shard_map/all_gather | solution.py:71
  186.1 1.0 copy-start.1
Sparse Core Ops, SparseCore 0:
  37.0 61.5 all-gather.3
  101.9 78.7 all-gather.5

commit v2 on v1

--- a/solution.py
+++ b/solution.py
@@ -2,6 +2,7 @@
 import jax.numpy as jnp
 from jax import lax
 from jax.sharding import Mesh, PartitionSpec as P
+
 
 PANELS = 2
 LIVE_DEV = 256
@@ -9,6 +10,7 @@
 
 ROW = ("yh", "x", "core")
 COL = ("yl", "z")
+CHIP = ("yh", "x")
 
 modulus = 241.0
 half_modulus = 120.0
@@ -58,17 +60,22 @@
 
 
 def shards(pair_rows, reducers, pivots, counts):
-    row_index = lax.axis_index(ROW)
     col_index = lax.axis_index(COL)
     lower = lax.axis_index("yl")
+    core = lax.axis_index("core")
+    chip = lax.axis_index(CHIP)
+    chips = lax.axis_size(CHIP)
     col_width = pair_rows.shape[1]
     col_start = col_index * col_width
-    rows_dev = reducers.shape[1]
-    order = pivots.reshape(PANELS, -1, rows_dev).transpose(1, 0, 2).reshape(-1)
+    rows_dev = PANELS * reducers.shape[1]
+    order = pivots.reshape(PANELS, chips, 2, -1).transpose(2, 1, 0, 3).reshape(-1)
     total = order.shape[0]
-    own_cols = lax.dynamic_slice_in_dim(order, row_index * PANELS * rows_dev, PANELS * rows_dev)
-    normed = normalize_block(reducers.reshape(PANELS * rows_dev, col_width), own_cols, order, col_start)
-    panel = lax.all_gather(normed, ROW, axis=0, tiled=True)
+    half = total // 2
+    own_cols = lax.dynamic_slice_in_dim(order, core * half + chip * rows_dev, rows_dev)
+    normed = normalize_block(reducers.reshape(rows_dev, col_width), own_cols, order, col_start)
+    copies = jnp.broadcast_to(normed[None], (chips, rows_dev, col_width))
+    mine_panel = lax.all_to_all(copies, CHIP, 0, 0, tiled=True).reshape(half, col_width)
+    panels = (mine_panel, swap(mine_panel, "core"))
 
     live = compact_rows(pair_rows, counts)
 
@@ -78,7 +85,10 @@
     rank = jnp.sum((same & (ids[None, :] < ids[:, None])).astype(jnp.int32), axis=1)
     rounds = jnp.max(rank) // CAP + 1
     z_size = lax.axis_size("z")
-    slot = (owner % z_size) * (2 * CAP) + (owner // z_size) * CAP
+    slot = (owner % z_size) * (2 * CAP) + (owner // z_size) * CAP + rank
+    pairs = jnp.stack([rank, slot]).reshape(2, 2, half)
+    pairs = jnp.where(core == 0, pairs, pairs[:, ::-1])
+    my_rank, my_slot = pairs.reshape(2, total)
 
     def fetch(step):
         base = step * CAP
@@ -87,28 +97,28 @@
         local = jnp.sum(jnp.where(hit, order[None, :] - col_start + 1, 0), axis=1) - 1
         choose = (local[:, None] == lax.iota(jnp.int32, col_width)[None, :]).astype(jnp.bfloat16)
         mine = lax.dot_general(choose, live, (((1,), (1,)), ((), ())), preferred_element_type=jnp.float32)
-        mine = centered(mine).astype(jnp.bfloat16)
+        mine = centered(mine).astype(jnp.int16)
         theirs = swap(mine, "yl")
         both = jnp.where(lower == 0, jnp.stack([mine, theirs]), jnp.stack([theirs, mine]))
         spread = lax.all_gather(both.reshape(2 * CAP, LIVE_DEV), "z", axis=0, tiled=True)
-        inside = (rank >= base) & (rank < base + CAP)
-        got = jnp.take(spread, jnp.where(inside, slot + rank - base, 0), axis=0)
+        spread = spread.astype(jnp.bfloat16)
+        inside = (my_rank >= base) & (my_rank < base + CAP)
+        got = jnp.take(spread, jnp.where(inside, my_slot - base, 0), axis=0)
         return jnp.where(inside[:, None], got, jnp.zeros_like(got))
-
-    half = total // 2
 
     def reduce_by(result, factors):
         for part in range(2):
             product = lax.dot_general(
                 factors[part * half:(part + 1) * half],
-                panel[part * half:(part + 1) * half],
+                panels[part],
                 (((0,), (0,)), ((), ())),
                 preferred_element_type=jnp.float32,
             )
             result = jnp.mod(result - product, modulus)
         return result
 
-    first = reduce_by(live.astype(jnp.float32), fetch(0)).astype(jnp.int32)
+    factors = fetch(0)
+    first = reduce_by(live.astype(jnp.float32), factors).astype(jnp.int32)
     _, result = lax.while_loop(
         lambda state: state[0] < rounds,
         lambda state: (

time: 194 us -> 120 us (0.62)
  the two profiles are of different devices: /device:TPU:1 before, /device:TPU:6 now
where the time goes in v2:
time: 120 us; the launch traced here: 119 us
  blocking collectives  42.5 us (35%)
  waiting for transfers between devices  22.5 us (19%)
  other arithmetic  15.9 us (13%)
  starting transfers between devices  15.1 us (13%)
  local copies, waits for them, and re-layouts  13.9 us (12%)
  matrix products  5.32 us (4%)
  between operations  3.93 us (3%)
    all_gather x1, blocking collectives, fetch(): lax.all_gather(both.reshape(2 * CAP, LIVE_DEV), 'z', axis=0, tiled=True)  42.5 us
    all_to_all x1, waiting for transfers between devices, shards(): lax.all_to_all(copies, CHIP, 0, 0, tiled=True).reshape(half, col_width)  21 us
    all_to_all x1, starting transfers between devices, shards(): lax.all_to_all(copies, CHIP, 0, 0, tiled=True).reshape(half, col_width)  9.34 us
    gather x1, local copies, waits for them, and re-layouts, fetch(): got = jnp.take(spread, jnp.where(inside, my_slot - base, 0), axis=0)  8.25 us
    ppermute x3, starting transfers between devices, swap(): return lax.ppermute(value, axis, [(0, 1), (1, 0)])  5.74 us
    dot_general x2, matrix products, reduce_by(): lax.dot_general(factors[part * half:(part + 1) * half], panels[part], (((...  5.01 us
    reduce_sum x1, other arithmetic, shards(): jnp.sum((same & (ids[None, :] < ids[:, None])).astype(jnp.int32), axis=1)  4.46 us
    gather x2, local copies, waits for them, and re-layouts, take_window(): return jnp.take(source, jnp.clip(index, 0, source.shape[0] - 1), axis=0)  3.15 us
  transfers between devices with their start and end apart: 4, of which 2 were waited for; matrix products, arithmetic and copies ran while one was open for 21% of the time, Pallas kernels for 0%

profile of v2, /device:TPU:6, one launch (start us, length us, event | category | flops | bytes accessed | tf_op | source)
XLA Modules:
  0.0 119.2 jit_solution(13418345876680603428)
XLA Ops:
  0.0 1.3 %fusion.28 = s32[]{:T(128)} fusion(s32[16]{0:T(128)} %param.11, s32[]{:T(128)S(6)} %sub.111), kind=kLoop, calls=%fused_computation.103 | loop fusion | flops 47 | bytes 72 | tf_op jit(solution)/shard_map/reduce_sum | solution.py:25
  1.9 1.8 %convert_convert_fusion = bf16[512,1024]{1,0:T(8,128)(2,1)S(1)} fusion(s32[512,1024]{1,0:T(8,128)} %param.8), kind=kLoop, calls=%fused_computation.34 | loop fusion | flops 1048576 | bytes 3145728 | tf_op jit(solution)/shard_map/convert_element_type | solution.py:41
  3.7 1.2 gather_fusion.3
  4.9 0.9 broadcast_select_fusion
  5.8 1.9 %collective-permute-start.1 = (bf16[256,1024]{1,0:T(8,128)(2,1)}, bf16[256,1024]{1,0:T(8,128)(2,1)}, u32[]{:S(2)}, u32[]{:S(2)}) collective-permute-start(bf16[256,1024]{1,0:T(8,128)(2,1)} %broadcast_select_fusion), channel_id=1, source_target_pairs={{0,32},{32,0},{1,33},{33,1},{2,34},{34,2},{3,35},{35,3},{4,36},{36... | collective-permute-start | bytes 1572872 | tf_op jit(solution)/shard_map/ppermute | solution.py:29
  8.0 1.2 compare_reduce_fusion
  9.3 1.6 %broadcast_in_dim.152 = bf16[8,128,1024]{2,1,0:T(8,128)(2,1)} broadcast(bf16[128,1024]{1,0:T(8,128)(2,1)S(1)} %fusion.19), dimensions={1,2} | broadcast | bytes 2359296 | tf_op jit(solution)/shard_map/broadcast_in_dim | solution.py:76
  10.9 9.3 %all-to-all-start = ((bf16[8,128,1024]{2,1,0:T(8,128)(2,1)}), bf16[8,128,1024]{2,1,0:T(8,128)(2,1)S(1)}, u32[]{:S(2)}, u32[]{:S(2)}) async-start(bf16[8,128,1024]{2,1,0:T(8,128)(2,1)} %broadcast_in_dim.152), calls=%async_computation | async-start | bytes 4194304 | tf_op jit(solution)/shard_map/all_to_all | solution.py:77
  21.5 2.0 %gather_fusion.2 = bf16[256,1024]{1,0:T(8,128)(2,1)} fusion(bf16[512,1024]{1,0:T(8,128)(2,1)S(1)} %convert_convert_fusion, s32[1024]{0:T(1024)S(1)} %pad_clamp_fusion.1), kind=kCustom, calls=%fused_computation.clone | custom fusion | bytes 1049600 | tf_op jit(solution)/shard_map/jit(_take)/gather | solution.py:34
  23.5 4.5 %convert_reduce_fusion = s32[2048]{0:T(1024)S(1)} fusion(s32[2048]{0:T(1024)S(1)} %get-tuple-element.368), kind=kLoop, calls=%fused_computation.30 | loop fusion | flops 20969472 | bytes 16384 | tf_op jit(solution)/shard_map/reduce_sum | solution.py:85
  28.7 0.6 compare_and_fusion.5
  29.3 1.3 %select_select_fusion.2 = bf16[256,1024]{1,0:T(8,128)(2,1)S(1)} fusion(bf16[256,1024]{1,0:T(8,128)(2,1)} %collective-permute-done.1, bf16[256,1024]{1,0:T(8,128)(2,1)} %gather_fusion.2, pred[256]{0:T(512)(128)(4,1)S(1)} %get-tuple-element.265, pred[256]{0:T(512)(128)(4,1)S(1)} %get-tuple-element.266), kind=kLoop, calls=%fused_computation.53 | loop fusion | flops 524288 | bytes 1573376 | tf_op jit(solution)/shard_map/jit(_where)/select_n | solution.py:48
  30.6 21.0 %all-to-all-done = bf16[8,128,1024]{2,1,0:T(8,128)(2,1)S(1)} async-done(((bf16[8,128,1024]{2,1,0:T(8,128)(2,1)}), bf16[8,128,1024]{2,1,0:T(8,128)(2,1)S(1)}, u32[]{:S(2)}, u32[]{:S(2)}) %all-to-all-start) | async-done | bytes 2097184 | tf_op jit(solution)/shard_map/all_to_all | solution.py:77
  51.6 1.9 %collective-permute-start.3 = (bf16[1024,1024]{1,0:T(8,128)(2,1)S(1)}, bf16[1024,1024]{1,0:T(8,128)(2,1)}, u32[]{:S(2)}, u32[]{:S(2)}) collective-permute-start(bf16[1024,1024]{1,0:T(8,128)(2,1)S(1)} %bitcast.59), channel_id=1, source_target_pairs={{0,32},{32,0},{1,33},{33,1},{2,34},{34,2},{3,35},{35,3},{4,36},{36... | collective-permute-start | bytes 6291464 | tf_op jit(solution)/shard_map/ppermute | solution.py:29
  53.5 0.3 subtract_convert_fusion.1
  53.8 1.9 %collective-permute-start.2 = (s16[96,256]{1,0:T(8,128)(2,1)S(1)}, s16[96,256]{1,0:T(8,128)(2,1)S(1)}, u32[]{:S(2)}, u32[]{:S(2)}) collective-permute-start(s16[96,256]{1,0:T(8,128)(2,1)S(1)} %subtract_convert_fusion.1), channel_id=1, source_target_pairs={{0,16},{16,0},{1,17},{17,1},{2,18},{18,2},{3,19},{19,3},{4,20},{20... | collective-permute-start | bytes 147464 | tf_op jit(solution)/shard_map/ppermute | solution.py:29
  55.8 0.6 reduce_max.9
  58.4 1.5 %collective-permute-done.2 = s16[96,256]{1,0:T(8,128)(2,1)S(1)} collective-permute-done((s16[96,256]{1,0:T(8,128)(2,1)S(1)}, s16[96,256]{1,0:T(8,128)(2,1)S(1)}, u32[]{:S(2)}, u32[]{:S(2)}) %collective-permute-start.2) | collective-permute-done | bytes 49184 | tf_op jit(solution)/shard_map/ppermute | solution.py:29
  59.9 42.5 %all-gather.2 = s16[3072,256]{1,0:T(8,128)(2,1)S(1)} all-gather(s16[192,256]{1,0:T(8,128)(2,1)S(1)} %bitcast.67), channel_id=1, replica_groups=mesh['yh'=2,'x'=4,'core'=2,'yl'=2,'z'=16] {'z'}, dimensions={0}, use_global_device_ids=true | all-gather | bytes 1671168 | tf_op jit(solution)/shard_map/all_gather | solution.py:103
  102.4 1.7 %convert_element_type.72 = bf16[3072,256]{1,0:T(8,128)(2,1)} convert(s16[3072,256]{1,0:T(8,128)(2,1)S(1)} %all-gather.2) | non-fusion elementwise | flops 786432 | bytes 3145728 | tf_op jit(solution)/shard_map/convert_element_type | solution.py:104
  104.1 8.2 %gather_fusion.1 = bf16[2048,256]{1,0:T(8,128)(2,1)S(1)} fusion(bf16[3072,256]{1,0:T(8,128)(2,1)} %convert_element_type.72, s32[2048]{0:T(1024)S(1)} %broadcast_clamp_fusion.1), kind=kCustom, calls=%fused_computation.3 | custom fusion | bytes 2105344 | tf_op jit(solution)/shard_map/jit(_take)/gather | solution.py:106
  112.4 1.5 %select_select_fusion.1 = bf16[2048,256]{1,0:T(8,128)(2,1)S(1)} fusion(bf16[2048,256]{1,0:T(8,128)(2,1)S(1)} %gather_fusion.1, pred[2048]{0:T(1024)(128)(4,1)S(1)} %get-tuple-element.258, pred[2048]{0:T(1024)(128)(4,1)S(1)} %get-tuple-element.259), kind=kLoop, calls=%fused_computation.41 | loop fusion | flops 1048576 | bytes 2101248 | tf_op jit(solution)/shard_map/jit(_where)/select_n | solution.py:107
  113.9 0.7 fusion.16
  114.9 4.3 %fusion.10 = s32[256,1024]{1,0:T(8,128)} fusion(f32[256,1024]{1,0:T(8,128)S(1)} %fusion.16, bf16[256,1024]{1,0:T(8,128)(2,1)S(1)} %copy-done.5, bf16[1024,1024]{1,0:T(8,128)(2,1)} %collective-permute-done.3, bf16[2048,256]{1,0:T(8,128)(2,1)S(1)} %select_select_fusion.1), kind=kOutput, calls=%fused_computation.39 | convolution fusion | flops 541065216 | bytes 5242880 | tf_op jit(solution)/shard_map/dot_general | solution.py:111
  (39 shorter events, 1.5 us)
Async XLA Ops:
  3.7 4.0 %copy-start.7 = (s32[2,1024]{1,0:T(2,128)S(1)}, s32[2,1024]{1,0:T(2,128)}, u32[]{:S(2)}) copy-start(s32[2,1024]{1,0:T(2,128)} %param.10) | copy-start | bytes 24580
  3.7 5.5 %copy-start.3 = (s32[2,64,1024]{2,1,0:T(8,128)S(1)}, s32[2,64,1024]{2,1,0:T(8,128)}, u32[]{:S(2)}) copy-start(s32[2,64,1024]{2,1,0:T(8,128)} %param.9) | copy-start | bytes 1572868
  5.8 23.4 %collective-permute-start.1 = (bf16[256,1024]{1,0:T(8,128)(2,1)}, bf16[256,1024]{1,0:T(8,128)(2,1)}, u32[]{:S(2)}, u32[]{:S(2)}) collective-permute-start(bf16[256,1024]{1,0:T(8,128)(2,1)} %broadcast_select_fusion), channel_id=1, source_target_pairs={{0,32},{32,0},{1,33},{33,1},{2,34},{34,2},{3,35},{35,3},{4,36},{36... | collective-permute-start | bytes 1572872 | tf_op jit(solution)/shard_map/ppermute | solution.py:29
  10.9 40.7 %all-to-all-start = ((bf16[8,128,1024]{2,1,0:T(8,128)(2,1)}), bf16[8,128,1024]{2,1,0:T(8,128)(2,1)S(1)}, u32[]{:S(2)}, u32[]{:S(2)}) async-start(bf16[8,128,1024]{2,1,0:T(8,128)(2,1)} %broadcast_in_dim.152), calls=%async_computation | async-start | bytes 4194304 | tf_op jit(solution)/shard_map/all_to_all | solution.py:77
  30.6 71.8 %copy-start.4 = (bf16[256,1024]{1,0:T(8,128)(2,1)}, bf16[256,1024]{1,0:T(8,128)(2,1)S(1)}, u32[]{:S(2)}) copy-start(bf16[256,1024]{1,0:T(8,128)(2,1)S(1)} %select_select_fusion.2) | copy-start | bytes 1572868
  51.6 63.0 %collective-permute-start.3 = (bf16[1024,1024]{1,0:T(8,128)(2,1)S(1)}, bf16[1024,1024]{1,0:T(8,128)(2,1)}, u32[]{:S(2)}, u32[]{:S(2)}) collective-permute-start(bf16[1024,1024]{1,0:T(8,128)(2,1)S(1)} %bitcast.59), channel_id=1, source_target_pairs={{0,32},{32,0},{1,33},{33,1},{2,34},{34,2},{3,35},{35,3},{4,36},{36... | collective-permute-start | bytes 6291464 | tf_op jit(solution)/shard_map/ppermute | solution.py:29
  53.8 6.0 %collective-permute-start.2 = (s16[96,256]{1,0:T(8,128)(2,1)S(1)}, s16[96,256]{1,0:T(8,128)(2,1)S(1)}, u32[]{:S(2)}, u32[]{:S(2)}) collective-permute-start(s16[96,256]{1,0:T(8,128)(2,1)S(1)} %subtract_convert_fusion.1), channel_id=1, source_target_pairs={{0,16},{16,0},{1,17},{17,1},{2,18},{18,2},{3,19},{19,3},{4,20},{20... | collective-permute-start | bytes 147464 | tf_op jit(solution)/shard_map/ppermute | solution.py:29
  113.9 1.0 copy-start.5

commit v3 on v2

v3 whole, which is shorter than its diff:
```python
import jax
import jax.numpy as jnp
from jax import lax
from jax.experimental import pallas as pl
from jax.experimental.pallas import tpu as pltpu
from jax.sharding import Mesh, PartitionSpec as P


PANELS = 2
LIVE_DEV = 256
CAP = 96
LANES = 128

ROW = ("yh", "x", "core")
COL = ("yl", "z")
CHIP = ("yh", "x")

modulus = 241.0
half_modulus = 120.0

NN = (((1,), (0,)), ((), ()))
NT = (((1,), (1,)), ((), ()))


def centered(values):
    return values - modulus * (values > half_modulus).astype(values.dtype)


def remainder(values):
    rest = values - modulus * jnp.floor(values * (1.0 / modulus))
    rest = jnp.where(rest < 0.0, rest + modulus, rest)
    return jnp.where(rest >= modulus, rest - modulus, rest)


def swap(value, axis):
    return lax.ppermute(value, axis, [(0, 1), (1, 0)])


def dot(left, right, dims):
    return lax.dot_general(left, right, dims, preferred_element_type=jnp.float32)


def spread_row(grid):
    return jnp.concatenate([grid[i:i + 1] for i in range(grid.shape[0])], axis=1)


def front_kernel(counts, pivots, rows, reducers, normed, kept, sent, slots):
    width = rows.shape[1]
    groups = width // LANES
    core = lax.axis_index("core")
    owner = (lax.axis_index("yh") * 4 + lax.axis_index("x")) * 2 + core
    start = (lax.axis_index("yl") * 16 + lax.axis_index("z")) * width

    count = pivots.shape[1]
    lane_rows = lax.broadcasted_iota(jnp.int32, (LANES, count), 0)
    group_rows = lax.broadcasted_iota(jnp.int32, (groups, count), 0)
    marks = jnp.zeros((groups, LANES), jnp.float32)
    for panel in range(PANELS):
        place = pivots[panel:panel + 1, :] - start
        high = jnp.where((place >= 0) & (place < width), place >> 7, -1)
        marks += dot(
            (group_rows == high).astype(jnp.float32).astype(jnp.bfloat16),
            (lane_rows == (place & (LANES - 1))).astype(jnp.float32).astype(jnp.bfloat16),
            NT,
        )
    flags = marks.astype(jnp.bfloat16)
    lower = lax.broadcasted_iota(jnp.int32, (LANES, LANES), 0)
    upper = lax.broadcasted_iota(jnp.int32, (LANES, LANES), 1)
    inside = dot(flags, (lower < upper).astype(jnp.float32).astype(jnp.bfloat16), NN)
    totals = dot(flags, jnp.ones((LANES, LANES), jnp.bfloat16), NN)
    before = jnp.zeros((groups, LANES), jnp.float32)
    group_ids = lax.broadcasted_iota(jnp.int32, (groups, LANES), 0)
    for group in range(groups - 1):
        before += jnp.where(group_ids > group, totals[group:group + 1], 0.0)
    slots[...] = spread_row(jnp.where(marks > 0.0, inside + before, -1.0))

    rows_dev = reducers.shape[0]
    part = rows_dev // PANELS
    own = pivots[:, pl.ds(pl.multiple_of((owner // 2) * LANES, LANES), LANES)].astype(jnp.float32)
    row_ids = lax.broadcasted_iota(jnp.int32, (rows_dev, LANES), 0)
    lane_ids = lax.broadcasted_iota(jnp.int32, (rows_dev, LANES), 1)
    chosen = jnp.where(row_ids < part, own[0:1], own[1:2])
    target = (row_ids & (part - 1)) + part * core
    own_pivot = jnp.sum(jnp.where(lane_ids == target, chosen, 0.0), axis=1, keepdims=True)
    base = start.astype(jnp.float32)
    for group in range(groups):
        cols = slice(group * LANES, (group + 1) * LANES)
        here = (lane_ids + group * LANES).astype(jnp.float32) + base
        entries = centered(reducers[:, cols].astype(jnp.float32))
        pivot_value = jnp.where(here == own_pivot, 1.0, 0.0)
        normed[:, cols] = jnp.where(marks[group:group + 1] > 0.0, pivot_value, entries).astype(jnp.bfloat16)

    first = counts[owner - core]
    mine = counts[owner]
    capacity = rows.shape[0]
    values = rows[...].astype(jnp.float32).astype(jnp.bfloat16)
    slot_ids = lax.broadcasted_iota(jnp.int32, (LIVE_DEV, capacity), 1)
    places = lax.broadcasted_iota(jnp.int32, (LIVE_DEV, capacity), 0)
    live = slot_ids < mine
    for offset, out in ((core * (LIVE_DEV - first), kept), (jnp.where(core == 0, LIVE_DEV, -first), sent)):
        pick = (live & (slot_ids == places + offset)).astype(jnp.float32).astype(jnp.bfloat16)
        out[...] = dot(pick, values, NN).astype(jnp.bfloat16)


def extract_kernel(base, slots, kept, incoming, live, packed):
    width = kept.shape[1]
    values = (kept[...].astype(jnp.float32) + incoming[...].astype(jnp.float32)).astype(jnp.bfloat16)
    live[...] = values
    want = (lax.broadcasted_iota(jnp.int32, (CAP, width), 0) + base[0]).astype(jnp.float32)
    choose = (slots[...] == want).astype(jnp.float32).astype(jnp.bfloat16)
    packed[...] = centered(dot(choose, values, NT)).astype(jnp.int32).astype(jnp.int16)


VMEM = pl.BlockSpec(memory_space=pltpu.VMEM)
SMEM = pl.BlockSpec(memory_space=pltpu.SMEM)


def front(counts, pivots, rows, reducers):
    width = rows.shape[1]
    return pl.pallas_call(
        front_kernel,
        out_shape=(
            jax.ShapeDtypeStruct(reducers.shape, jnp.bfloat16),
            jax.ShapeDtypeStruct((LIVE_DEV, width), jnp.bfloat16),
            jax.ShapeDtypeStruct((LIVE_DEV, width), jnp.bfloat16),
            jax.ShapeDtypeStruct((1, width), jnp.float32),
        ),
        in_specs=[SMEM, VMEM, VMEM, VMEM],
        out_specs=(VMEM,) * 4,
        name="front",
    )(counts, pivots, rows, reducers)


def extract(base, slots, kept, incoming):
    return pl.pallas_call(
        extract_kernel,
        out_shape=(
            jax.ShapeDtypeStruct(kept.shape, jnp.bfloat16),
            jax.ShapeDtypeStruct((CAP, LIVE_DEV), jnp.int16),
        ),
        in_specs=[SMEM, VMEM, VMEM, VMEM],
        out_specs=(VMEM,) * 2,
        name="extract",
    )(base, slots, kept, incoming)


def shards(pair_rows, reducers, pivots, counts):
    lower = lax.axis_index("yl")
    core = lax.axis_index("core")
    chips = lax.axis_size(CHIP)
    z_size = lax.axis_size("z")
    col_width = pair_rows.shape[1]
    rows_dev = PANELS * reducers.shape[1]
    normed, kept, sent, slots = front(counts, pivots, pair_rows, reducers.reshape(rows_dev, col_width))
    incoming = swap(sent, "core")

    order = pivots.reshape(PANELS, chips, 2, -1).transpose(2, 1, 0, 3).reshape(-1)
    total = order.shape[0]
    half = total // 2
    copies = jnp.broadcast_to(normed[None], (chips, rows_dev, col_width))
    mine_panel = lax.all_to_all(copies, CHIP, 0, 0, tiled=True).reshape(half, col_width)
    panels = (mine_panel, swap(mine_panel, "core"))

    owner = order // col_width
    same = owner[:, None] == owner[None, :]
    rank = jnp.sum((same & (order[None, :] < order[:, None])).astype(jnp.int32), axis=1)
    rounds = jnp.max(rank) // CAP + 1
    slot = (owner % z_size) * (2 * CAP) + (owner // z_size) * CAP + rank
    pairs = jnp.stack([rank, slot]).reshape(2, 2, half)
    pairs = jnp.where(core == 0, pairs, pairs[:, ::-1])
    my_rank, my_slot = pairs.reshape(2, total)

    def fetch(step, kept, incoming):
        base = step * CAP
        live, mine = extract(base.reshape(1), slots, kept, incoming)
        theirs = swap(mine, "yl")
        both = jnp.where(lower == 0, jnp.stack([mine, theirs]), jnp.stack([theirs, mine]))
        spread = lax.all_gather(both.reshape(2 * CAP, LIVE_DEV), "z", axis=0, tiled=True)
        here = jnp.where((my_rank >= base) & (my_rank < base + CAP), my_slot - base, -1)
        table = (here[:, None] == lax.iota(jnp.int32, spread.shape[0])[None, :]).astype(jnp.bfloat16)
        factors = dot(table, spread.astype(jnp.bfloat16), NN)
        return live, factors.astype(jnp.bfloat16)

    def reduce_by(result, factors):
        for part in range(2):
            product = dot(factors[part * half:(part + 1) * half], panels[part], (((0,), (0,)), ((), ())))
            result = remainder(result - product)
        return result

    live, factors = fetch(jnp.int32(0), kept, incoming)
    first = reduce_by(live.astype(jnp.float32), factors).astype(jnp.int32)

    def another(state):
        step, result = state
        _, factors = fetch(step, kept, incoming)
        return step + 1, reduce_by(result.astype(jnp.float32), factors).astype(jnp.int32)

    _, result = lax.while_loop(lambda state: state[0] < rounds, another, (jnp.int32(1), first))
    return result


def solution(mesh):
    fine = Mesh(mesh.devices.reshape(2, 4, 2, 2, 16), (*ROW, *COL))
    return jax.shard_map(
        shards,
        mesh=fine,
        in_specs=(P(ROW, COL), P(None, ROW, COL), P(), P()),
        out_specs=P(ROW, COL),
        check_vma=False,
    )
```

time: 120 us -> 104 us (0.87)
  other arithmetic: 15.9 us -> 5.15 us
  local copies, waits for them, and re-layouts: 13.9 us -> 4.34 us
  Pallas kernels: 0 us -> 4.86 us
  matrix products: 5.32 us -> 7.13 us
  waiting for transfers between devices: 22.5 us -> 20.7 us
  between operations: 3.93 us -> 2.29 us
    gather x3 -> x0, local copies, waits for them, and re-layouts: 11.4 us -> none  [the longest x1 8.25 us: fetch(): got = jnp.take(spread, jnp.where(inside, my_slot - base, 0), axis=0)]
    pallas_call x0 -> x2, Pallas kernels: none -> 4.86 us  [the longest x1 3.83 us: front(): pl.pallas_call(front_kernel, out_shape=(jax.ShapeDtypeStruct(reducers.sha...]
    select_n x6 -> x2, other arithmetic: 3.76 us -> 0.01 us  [the longest x1 0.01 us: shards(): owner = order // col_width]
    convert_element_type x3 -> x0, other arithmetic: 3.65 us -> none  [the longest x1 1.83 us: compact_rows(): slots = pair_rows.astype(jnp.float32).astype(jnp.bfloat16)]
    all_to_all x1, waiting for transfers between devices: 21 us -> 17.7 us  [shards(): lax.all_to_all(copies, CHIP, 0, 0, tiled=True).reshape(half, col_width)]
    reduce_sum x3 -> x1, other arithmetic: 5.98 us -> 3.45 us  [shards(): jnp.sum((same & (order[None, :] < order[:, None])).astype(jnp.int32), axi...]
    dot_general x3, matrix products: 5.32 us -> 7.13 us  [dot(): lax.dot_general(left, right, dims, preferred_element_type=jnp.float32)]
    ppermute x3, waiting for transfers between devices: 1.5 us -> 3.03 us  [swap(): return lax.ppermute(value, axis, [(0, 1), (1, 0)])]
  transfers between devices with their start and end apart: 4 -> 4, of which waited for: 2 -> 2; matrix products, arithmetic and copies ran while one was open for 21% -> 14% of each run, Pallas kernels for 0% -> 1%
where the time goes in v3:
time: 104 us; the launch traced here: 103 us
  blocking collectives  43.4 us (42%)
  waiting for transfers between devices  20.7 us (20%)
  starting transfers between devices  15.2 us (15%)
  matrix products  7.13 us (7%)
  other arithmetic  5.15 us (5%)
  Pallas kernels  4.86 us (5%)
  local copies, waits for them, and re-layouts  4.34 us (4%)
  between operations  2.29 us (2%)
    all_gather x1, blocking collectives, fetch(): lax.all_gather(both.reshape(2 * CAP, LIVE_DEV), 'z', axis=0, tiled=True)  43.4 us
    all_to_all x1, waiting for transfers between devices, shards(): lax.all_to_all(copies, CHIP, 0, 0, tiled=True).reshape(half, col_width)  17.7 us
    all_to_all x1, starting transfers between devices, shards(): lax.all_to_all(copies, CHIP, 0, 0, tiled=True).reshape(half, col_width)  9.47 us
    dot_general x3, matrix products, dot(): lax.dot_general(left, right, dims, preferred_element_type=jnp.float32)  7.13 us
    ppermute x3, starting transfers between devices, swap(): return lax.ppermute(value, axis, [(0, 1), (1, 0)])  5.72 us
    pallas_call x1, Pallas kernels, front(): pl.pallas_call(front_kernel, out_shape=(jax.ShapeDtypeStruct(reducers.sha...  3.83 us
    reduce_sum x1, other arithmetic, shards(): jnp.sum((same & (order[None, :] < order[:, None])).astype(jnp.int32), axi...  3.45 us
    ppermute x3, waiting for transfers between devices, swap(): return lax.ppermute(value, axis, [(0, 1), (1, 0)])  3.03 us
  transfers between devices with their start and end apart: 4, of which 2 were waited for; matrix products, arithmetic and copies ran while one was open for 14% of the time, Pallas kernels for 1%

profile of v3, /device:TPU:6, one launch (start us, length us, event | category | flops | bytes accessed | tf_op | source)
XLA Modules:
  0.0 103.3 jit_solution(9391100995601299127)
XLA Ops:
  0.0 3.8 %front.1 = (bf16[128,1024]{1,0:T(8,128)(2,1)}, bf16[256,1024]{1,0:T(8,128)(2,1)S(1)}, bf16[256,1024]{1,0:T(8,128)(2,1)}, f32[1,1024]{1,0:T(1,128)S(1)}) custom-call(s32[16]{0:T(128)} %counts.1, s32[2,1024]{1,0:T(2,128)} %pivots.1, s32[512,1024]{1,0:T(8,128)} %rows.1, s32[128,1024]{1,0:T(8,128)} %bitcast.46), custom_call_target="tpu_custom_call" | custom-call | tf_op jit(solution)/shard_map/front/pallas_call | solution.py:120
  3.8 1.9 %collective-permute-start.1 = (bf16[256,1024]{1,0:T(8,128)(2,1)}, bf16[256,1024]{1,0:T(8,128)(2,1)S(1)}, u32[]{:S(2)}, u32[]{:S(2)}) collective-permute-start(bf16[256,1024]{1,0:T(8,128)(2,1)} %get-tuple-element.184), channel_id=1, source_target_pairs={{0,32},{32,0},{1,33},{33,1},{2,34},{34,2},{3,35},{35,3},{4,36},{36... | collective-permute-start | bytes 1572872 | tf_op jit(solution)/shard_map/ppermute | solution.py:36
  5.7 2.5 %broadcast_in_dim.6 = bf16[8,128,1024]{2,1,0:T(8,128)(2,1)} broadcast(bf16[128,1024]{1,0:T(8,128)(2,1)} %get-tuple-element.187), dimensions={1,2} | broadcast | bytes 2359296 | tf_op jit(solution)/shard_map/broadcast_in_dim | solution.py:160
  8.3 9.5 %all-to-all-start = ((bf16[8,128,1024]{2,1,0:T(8,128)(2,1)}), bf16[8,128,1024]{2,1,0:T(8,128)(2,1)S(1)}, u32[]{:S(2)}, u32[]{:S(2)}) async-start(bf16[8,128,1024]{2,1,0:T(8,128)(2,1)} %broadcast_in_dim.6), calls=%async_computation | async-start | bytes 4194304 | tf_op jit(solution)/shard_map/all_to_all | solution.py:161
  17.8 0.1 reshape.285
  17.9 0.1 reshape.286
  17.9 0.1 reshape.287
  18.0 3.5 %convert_reduce_fusion = s32[2048]{0:T(1024)S(1)} fusion(s32[2048]{0:T(1024)S(1)} %reshape.286, s32[2048]{0:T(1024)S(1)} %add_select_fusion.2), kind=kLoop, calls=%fused_computation.18 | loop fusion | flops 20969472 | bytes 24576 | tf_op jit(solution)/shard_map/reduce_sum | solution.py:166
  21.5 0.1 fusion.18
  21.6 0.2 rev.3
  21.9 1.0 %extract.6 = (bf16[256,1024]{1,0:T(8,128)(2,1)}, s16[96,256]{1,0:T(8,128)(2,1)}) custom-call(s32[1]{0:T(128)} %constant.103.clone.1.base, f32[1,1024]{1,0:T(1,128)S(1)} %get-tuple-element.291.slots, bf16[256,1024]{1,0:T(8,128)(2,1)S(1)} %get-tuple-element.292.kept, bf16[256,1024]{1,0:T(8,128)(2,1)S(1)} %collective-permute-done.1.incoming), custom_call_target="tpu_custom_call" | custom-call | tf_op jit(solution)/shard_map/extract/pallas_call | solution.py:135
  23.0 1.9 %collective-permute-start.2 = (s16[96,256]{1,0:T(8,128)(2,1)}, s16[96,256]{1,0:T(8,128)(2,1)S(1)}, u32[]{:S(2)}, u32[]{:S(2)}) collective-permute-start(s16[96,256]{1,0:T(8,128)(2,1)} %get-tuple-element.186), channel_id=1, source_target_pairs={{0,16},{16,0},{1,17},{17,1},{2,18},{18,2},{3,19},{19,3},{4,20},{20... | collective-permute-start | bytes 147464 | tf_op jit(solution)/shard_map/ppermute | solution.py:36
  24.9 0.7 reduce_max.9
  27.7 3.0 %collective-permute-done.2 = s16[96,256]{1,0:T(8,128)(2,1)S(1)} collective-permute-done((s16[96,256]{1,0:T(8,128)(2,1)}, s16[96,256]{1,0:T(8,128)(2,1)S(1)}, u32[]{:S(2)}, u32[]{:S(2)}) %collective-permute-start.2) | collective-permute-done | bytes 49184 | tf_op jit(solution)/shard_map/ppermute | solution.py:36
  30.7 0.9 add_select_fusion.1
  31.6 17.7 %all-to-all-done = bf16[8,128,1024]{2,1,0:T(8,128)(2,1)S(1)} async-done(((bf16[8,128,1024]{2,1,0:T(8,128)(2,1)}), bf16[8,128,1024]{2,1,0:T(8,128)(2,1)S(1)}, u32[]{:S(2)}, u32[]{:S(2)}) %all-to-all-start) | async-done | bytes 2097184 | tf_op jit(solution)/shard_map/all_to_all | solution.py:161
  49.3 1.9 %collective-permute-start.3 = (bf16[1024,1024]{1,0:T(8,128)(2,1)S(1)}, bf16[1024,1024]{1,0:T(8,128)(2,1)S(1)}, u32[]{:S(2)}, u32[]{:S(2)}) collective-permute-start(bf16[1024,1024]{1,0:T(8,128)(2,1)S(1)} %bitcast.40), channel_id=1, source_target_pairs={{0,32},{32,0},{1,33},{33,1},{2,34},{34,2},{3,35},{35,3},{4,36},{36... | collective-permute-start | bytes 6291464 | tf_op jit(solution)/shard_map/ppermute | solution.py:36
  51.2 43.4 %all-gather.2 = s16[3072,256]{1,0:T(8,128)(2,1)S(1)} all-gather(s16[192,256]{1,0:T(8,128)(2,1)S(1)} %bitcast.47), channel_id=1, replica_groups=mesh['yh'=2,'x'=4,'core'=2,'yl'=2,'z'=16] {'z'}, dimensions={0}, use_global_device_ids=true | all-gather | bytes 1671168 | tf_op jit(solution)/shard_map/all_gather | solution.py:178
  94.6 5.0 %fusion.9 = bf16[2048,256]{1,0:T(8,128)(2,1)S(1)} fusion(s32[2048]{0:T(1024)S(1)} %and_select_fusion.3, s16[3072,256]{1,0:T(8,128)(2,1)S(1)} %all-gather.2), kind=kOutput, calls=%fused_computation.24 | convolution fusion | flops 3228827648 | bytes 2629632 | tf_op jit(solution)/shard_map/dot_general | solution.py:40
  99.7 0.7 fusion.13
  100.4 0.3 copy-done.6
  100.7 1.4 %fusion.11 = s32[256,1024]{1,0:T(8,128)S(1)} fusion(bf16[1024,1024]{1,0:T(8,128)(2,1)S(1)} %collective-permute-done.3, f32[256,1024]{1,0:T(8,128)S(1)} %fusion.13, bf16[256,1024]{1,0:T(8,128)(2,1)S(1)} %copy-done.6, bf16[2048,256]{1,0:T(8,128)(2,1)S(1)} %fusion.9), kind=kOutput, calls=%fused_computation.27 | convolution fusion | flops 543162368 | bytes 5242880 | tf_op jit(solution)/shard_map/dot_general | solution.py:40
  102.1 0.2 while.13
  102.3 1.0 copy-done
  (20 shorter events, 0.1 us)
Async XLA Ops:
  3.8 18.1 %copy-start.1 = (bf16[256,1024]{1,0:T(8,128)(2,1)}, bf16[256,1024]{1,0:T(8,128)(2,1)S(1)}, u32[]{:S(2)}) copy-start(bf16[256,1024]{1,0:T(8,128)(2,1)S(1)} %get-tuple-element.292.kept) | copy-start | bytes 1572868
  3.8 18.1 %collective-permute-start.1 = (bf16[256,1024]{1,0:T(8,128)(2,1)}, bf16[256,1024]{1,0:T(8,128)(2,1)S(1)}, u32[]{:S(2)}, u32[]{:S(2)}) collective-permute-start(bf16[256,1024]{1,0:T(8,128)(2,1)} %get-tuple-element.184), channel_id=1, source_target_pairs={{0,32},{32,0},{1,33},{33,1},{2,34},{34,2},{3,35},{35,3},{4,36},{36... | collective-permute-start | bytes 1572872 | tf_op jit(solution)/shard_map/ppermute | solution.py:36
  8.3 9.5 %copy-start.3 = (s32[2,1024]{1,0:T(2,128)S(1)}, s32[2,1024]{1,0:T(2,128)}, u32[]{:S(2)}) copy-start(s32[2,1024]{1,0:T(2,128)} %pivots.1) | copy-start | bytes 24580
  8.3 41.0 %all-to-all-start = ((bf16[8,128,1024]{2,1,0:T(8,128)(2,1)}), bf16[8,128,1024]{2,1,0:T(8,128)(2,1)S(1)}, u32[]{:S(2)}, u32[]{:S(2)}) async-start(bf16[8,128,1024]{2,1,0:T(8,128)(2,1)} %broadcast_in_dim.6), calls=%async_computation | async-start | bytes 4194304 | tf_op jit(solution)/shard_map/all_to_all | solution.py:161
  21.9 77.7 %copy-start.2 = (bf16[256,1024]{1,0:T(8,128)(2,1)}, bf16[256,1024]{1,0:T(8,128)(2,1)S(1)}, u32[]{:S(2)}) copy-start(bf16[256,1024]{1,0:T(8,128)(2,1)S(1)} %collective-permute-done.1.incoming) | copy-start | bytes 1572868
  23.0 7.8 %collective-permute-start.2 = (s16[96,256]{1,0:T(8,128)(2,1)}, s16[96,256]{1,0:T(8,128)(2,1)S(1)}, u32[]{:S(2)}, u32[]{:S(2)}) collective-permute-start(s16[96,256]{1,0:T(8,128)(2,1)} %get-tuple-element.186), channel_id=1, source_target_pairs={{0,16},{16,0},{1,17},{17,1},{2,18},{18,2},{3,19},{19,3},{4,20},{20... | collective-permute-start | bytes 147464 | tf_op jit(solution)/shard_map/ppermute | solution.py:36
  49.3 51.1 %collective-permute-start.3 = (bf16[1024,1024]{1,0:T(8,128)(2,1)S(1)}, bf16[1024,1024]{1,0:T(8,128)(2,1)S(1)}, u32[]{:S(2)}, u32[]{:S(2)}) collective-permute-start(bf16[1024,1024]{1,0:T(8,128)(2,1)S(1)} %bitcast.40), channel_id=1, source_target_pairs={{0,32},{32,0},{1,33},{33,1},{2,34},{34,2},{3,35},{35,3},{4,36},{36... | collective-permute-start | bytes 6291464 | tf_op jit(solution)/shard_map/ppermute | solution.py:36
  99.7 1.0 %copy-start.6 = (bf16[256,1024]{1,0:T(8,128)(2,1)S(1)}, bf16[256,1024]{1,0:T(8,128)(2,1)}, u32[]{:S(2)}) copy-start(bf16[256,1024]{1,0:T(8,128)(2,1)} %get-tuple-element.185) | copy-start | bytes 1572868
  100.4 1.7 %copy-start.4 = (bf16[1024,1024]{1,0:T(8,128)(2,1)}, bf16[1024,1024]{1,0:T(8,128)(2,1)S(1)}, u32[]{:S(2)}) copy-start(bf16[1024,1024]{1,0:T(8,128)(2,1)S(1)} %collective-permute-done.3) | copy-start | bytes 6291460
  102.3 1.0 copy-start

commit v4 on v3

--- a/solution.py
+++ b/solution.py
@@ -44,7 +44,7 @@
     return jnp.concatenate([grid[i:i + 1] for i in range(grid.shape[0])], axis=1)
 
 
-def front_kernel(counts, pivots, rows, reducers, normed, kept, sent, slots):
+def front_kernel(counts, pivots, rows, reducers, copies, kept, sent, slots, normed, done):
     width = rows.shape[1]
     groups = width // LANES
     core = lax.axis_index("core")
@@ -89,6 +89,9 @@
         entries = centered(reducers[:, cols].astype(jnp.float32))
         pivot_value = jnp.where(here == own_pivot, 1.0, 0.0)
         normed[:, cols] = jnp.where(marks[group:group + 1] > 0.0, pivot_value, entries).astype(jnp.bfloat16)
+    writes = [pltpu.make_async_copy(normed, copies.at[chip], done.at[chip]) for chip in range(copies.shape[0])]
+    for write in writes:
+        write.start()
 
     first = counts[owner - core]
     mine = counts[owner]
@@ -100,13 +103,58 @@
     for offset, out in ((core * (LIVE_DEV - first), kept), (jnp.where(core == 0, LIVE_DEV, -first), sent)):
         pick = (live & (slot_ids == places + offset)).astype(jnp.float32).astype(jnp.bfloat16)
         out[...] = dot(pick, values, NN).astype(jnp.bfloat16)
-
-
-def extract_kernel(base, slots, kept, incoming, live, packed):
+    for write in writes:
+        write.wait()
+
+
+def ranks_kernel(pivots, ranks, slots, most):
+    core = lax.axis_index("core")
+    count = pivots.shape[1]
+    chunks = 32768 // LANES
+    lane_rows = lax.broadcasted_iota(jnp.int32, (LANES, count), 0)
+    chunk_rows = lax.broadcasted_iota(jnp.int32, (chunks, count), 0)
+    marks = jnp.zeros((chunks, LANES), jnp.float32)
+    chunk_marks, lane_marks = [], []
+    for panel in range(PANELS):
+        place = pivots[panel:panel + 1, :]
+        chunk_marks.append((chunk_rows == (place >> 7)).astype(jnp.float32).astype(jnp.bfloat16))
+        lane_marks.append(lane_rows == (place & (LANES - 1)))
+        marks += dot(chunk_marks[-1], lane_marks[-1].astype(jnp.float32).astype(jnp.bfloat16), NT)
+    flags = marks.astype(jnp.bfloat16)
+    lower = lax.broadcasted_iota(jnp.int32, (LANES, LANES), 0)
+    upper = lax.broadcasted_iota(jnp.int32, (LANES, LANES), 1)
+    inside = dot(flags, (lower < upper).astype(jnp.float32).astype(jnp.bfloat16), NN)
+    totals = dot(flags, jnp.ones((LANES, LANES), jnp.bfloat16), NN)
+    here = lax.broadcasted_iota(jnp.int32, (chunks, chunks), 0)
+    other = lax.broadcasted_iota(jnp.int32, (chunks, chunks), 1)
+    earlier = (((here >> 3) == (other >> 3)) & (other < here)).astype(jnp.float32).astype(jnp.bfloat16)
+    table = inside + dot(earlier, totals.astype(jnp.bfloat16), NN)
+    most[0] = jnp.max(jnp.where(marks > 0.0, table, 0.0)).astype(jnp.int32)
+    high = jnp.floor(table * (1.0 / 128.0))
+    low = (table - 128.0 * high).astype(jnp.bfloat16)
+    high = high.astype(jnp.bfloat16)
+    first_dims = (((0,), (0,)), ((), ()))
+    grids = []
+    for panel in range(PANELS):
+        found = 128.0 * dot(high, chunk_marks[panel], first_dims) + dot(low, chunk_marks[panel], first_dims)
+        rank = jnp.sum(jnp.where(lane_marks[panel], found, 0.0), axis=0, keepdims=True).astype(jnp.int32)
+        block = pivots[panel:panel + 1, :] >> 10
+        slot = (block & 15) * (2 * CAP) + (block >> 4) * CAP + rank
+        for value in (rank, slot):
+            grids.append(jnp.concatenate([value[:, i * LANES:(i + 1) * LANES] for i in range(count // LANES)], axis=0))
+    left = lax.broadcasted_iota(jnp.int32, grids[0].shape, 1) < LANES // 2
+    for out, a, b in ((ranks, grids[0], grids[2]), (slots, grids[1], grids[3])):
+        firsts = jnp.where(left, a, pltpu.roll(b, LANES // 2, axis=1))
+        seconds = jnp.where(left, pltpu.roll(a, LANES // 2, axis=1), b)
+        out[0] = jnp.where(core == 0, firsts, seconds)
+        out[1] = jnp.where(core == 0, seconds, firsts)
+
+
+def extract_kernel(slots, kept, incoming, live, packed):
     width = kept.shape[1]
     values = (kept[...].astype(jnp.float32) + incoming[...].astype(jnp.float32)).astype(jnp.bfloat16)
     live[...] = values
-    want = (lax.broadcasted_iota(jnp.int32, (CAP, width), 0) + base[0]).astype(jnp.float32)
+    want = lax.broadcasted_iota(jnp.int32, (CAP, width), 0).astype(jnp.float32)
     choose = (slots[...] == want).astype(jnp.float32).astype(jnp.bfloat16)
     packed[...] = centered(dot(choose, values, NT)).astype(jnp.int32).astype(jnp.int16)
 
@@ -115,71 +163,75 @@
 SMEM = pl.BlockSpec(memory_space=pltpu.SMEM)
 
 
-def front(counts, pivots, rows, reducers):
+def front(counts, pivots, rows, reducers, chips):
     width = rows.shape[1]
     return pl.pallas_call(
         front_kernel,
         out_shape=(
-            jax.ShapeDtypeStruct(reducers.shape, jnp.bfloat16),
+            jax.ShapeDtypeStruct((chips, *reducers.shape), jnp.bfloat16),
             jax.ShapeDtypeStruct((LIVE_DEV, width), jnp.bfloat16),
             jax.ShapeDtypeStruct((LIVE_DEV, width), jnp.bfloat16),
             jax.ShapeDtypeStruct((1, width), jnp.float32),
         ),
         in_specs=[SMEM, VMEM, VMEM, VMEM],
-        out_specs=(VMEM,) * 4,
+        out_specs=(pl.BlockSpec(memory_space=pl.ANY), VMEM, VMEM, VMEM),
+        scratch_shapes=[pltpu.VMEM(reducers.shape, jnp.bfloat16), pltpu.SemaphoreType.DMA((chips,))],
         name="front",
     )(counts, pivots, rows, reducers)
 
 
-def extract(base, slots, kept, incoming):
+def ranks(pivots):
+    grid = jax.ShapeDtypeStruct((2, pivots.shape[1] // LANES, LANES), jnp.int32)
+    return pl.pallas_call(
+        ranks_kernel,
+        out_shape=(grid, grid, jax.ShapeDtypeStruct((1,), jnp.int32)),
+        in_specs=[VMEM],
+        out_specs=(VMEM, VMEM, SMEM),
+        name="ranks",
+        compiler_params=pltpu.CompilerParams(vmem_limit_bytes=16 << 20),
+        cost_estimate=pl.CostEstimate(flops=2_000_000_000, bytes_accessed=1_000_000, transcendentals=0),
+    )(pivots)
+
+
+def extract(slots, kept, incoming):
     return pl.pallas_call(
         extract_kernel,
         out_shape=(
             jax.ShapeDtypeStruct(kept.shape, jnp.bfloat16),
             jax.ShapeDtypeStruct((CAP, LIVE_DEV), jnp.int16),
         ),
-        in_specs=[SMEM, VMEM, VMEM, VMEM],
+        in_specs=[VMEM, VMEM, VMEM],
         out_specs=(VMEM,) * 2,
         name="extract",
-    )(base, slots, kept, incoming)
+        compiler_params=pltpu.CompilerParams(vmem_limit_bytes=16 << 20),
+    )(slots, kept, incoming)
 
 
 def shards(pair_rows, reducers, pivots, counts):
     lower = lax.axis_index("yl")
-    core = lax.axis_index("core")
     chips = lax.axis_size(CHIP)
-    z_size = lax.axis_size("z")
     col_width = pair_rows.shape[1]
     rows_dev = PANELS * reducers.shape[1]
-    normed, kept, sent, slots = front(counts, pivots, pair_rows, reducers.reshape(rows_dev, col_width))
+    half = chips * rows_dev
+    copies, kept, sent, slots = front(counts, pivots, pair_rows, reducers.reshape(rows_dev, col_width), chips)
     incoming = swap(sent, "core")
-
-    order = pivots.reshape(PANELS, chips, 2, -1).transpose(2, 1, 0, 3).reshape(-1)
-    total = order.shape[0]
-    half = total // 2
-    copies = jnp.broadcast_to(normed[None], (chips, rows_dev, col_width))
-    mine_panel = lax.all_to_all(copies, CHIP, 0, 0, tiled=True).reshape(half, col_width)
-    panels = (mine_panel, swap(mine_panel, "core"))
-
-    owner = order // col_width
-    same = owner[:, None] == owner[None, :]
-    rank = jnp.sum((same & (order[None, :] < order[:, None])).astype(jnp.int32), axis=1)
-    rounds = jnp.max(rank) // CAP + 1
-    slot = (owner % z_size) * (2 * CAP) + (owner // z_size) * CAP + rank
-    pairs = jnp.stack([rank, slot]).reshape(2, 2, half)
-    pairs = jnp.where(core == 0, pairs, pairs[:, ::-1])
-    my_rank, my_slot = pairs.reshape(2, total)
-
-    def fetch(step, kept, incoming):
-        base = step * CAP
-        live, mine = extract(base.reshape(1), slots, kept, incoming)
+    my_rank, my_slot, most = ranks(pivots)
+    live, mine = extract(slots, kept, incoming)
+    my_rank, my_slot = my_rank.reshape(-1), my_slot.reshape(-1)
+    rounds = most[0] // CAP + 1
+
+    def gather(mine, base):
         theirs = swap(mine, "yl")
         both = jnp.where(lower == 0, jnp.stack([mine, theirs]), jnp.stack([theirs, mine]))
         spread = lax.all_gather(both.reshape(2 * CAP, LIVE_DEV), "z", axis=0, tiled=True)
         here = jnp.where((my_rank >= base) & (my_rank < base + CAP), my_slot - base, -1)
         table = (here[:, None] == lax.iota(jnp.int32, spread.shape[0])[None, :]).astype(jnp.bfloat16)
         factors = dot(table, spread.astype(jnp.bfloat16), NN)
-        return live, factors.astype(jnp.bfloat16)
+        return factors.astype(jnp.bfloat16)
+
+    mine_panel = lax.all_to_all(copies, CHIP, 0, 0, tiled=True).reshape(half, col_width)
+    factors = gather(mine, 0)
+    panels = (mine_panel, swap(mine_panel, "core"))
 
     def reduce_by(result, factors):
         for part in range(2):
@@ -187,13 +239,15 @@
             result = remainder(result - product)
         return result
 
-    live, factors = fetch(jnp.int32(0), kept, incoming)
     first = reduce_by(live.astype(jnp.float32), factors).astype(jnp.int32)
 
     def another(state):
         step, result = state
-        _, factors = fetch(step, kept, incoming)
-        return step + 1, reduce_by(result.astype(jnp.float32), factors).astype(jnp.int32)
+        base = step * CAP
+        want = (lax.iota(jnp.int32, CAP) + base).astype(jnp.float32)
+        choose = (slots == want[:, None]).astype(jnp.bfloat16)
+        more = centered(dot(choose, live, NT)).astype(jnp.int16)
+        return step + 1, reduce_by(result.astype(jnp.float32), gather(more, base)).astype(jnp.int32)
 
     _, result = lax.while_loop(lambda state: state[0] < rounds, another, (jnp.int32(1), first))
     return result

time: 104 us -> 97.1 us (0.934)
  waiting for transfers between devices: 20.7 us -> 15.1 us
  other arithmetic: 5.15 us -> 0.02 us
  blocking collectives: 43.4 us -> 47.5 us
  local copies, waits for them, and re-layouts: 4.34 us -> 1.27 us
  Pallas kernels: 4.86 us -> 7.85 us
    all_to_all x1, waiting for transfers between devices: 17.7 us -> 2.02 us  [shards(): lax.all_to_all(copies, CHIP, 0, 0, tiled=True).reshape(half, col_width)]
    ppermute x3, waiting for transfers between devices: 3.03 us -> 13.1 us  [swap(): return lax.ppermute(value, axis, [(0, 1), (1, 0)])]
    all_gather x1, blocking collectives: 43.4 us -> 47.5 us  [gather(): lax.all_gather(both.reshape(2 * CAP, LIVE_DEV), 'z', axis=0, tiled=True)]
    reduce_sum x1 -> x0, other arithmetic: 3.45 us -> none  [shards(): jnp.sum((same & (order[None, :] < order[:, None])).astype(jnp.int32), axi...]
    pallas_call x1 -> x2, Pallas kernels: 3.83 us -> 6.9 us  [the longest x1 4.7 us: front(): pl.pallas_call(front_kernel, out_shape=(jax.ShapeDtypeStruct((chips, *red...]
    broadcast_in_dim x1 -> x0, local copies, waits for them, and re-layouts: 2.54 us -> none  [shards(): copies = jnp.broadcast_to(normed[None], (chips, rows_dev, col_width))]
  transfers between devices with their start and end apart: 4 -> 4, of which waited for: 2 -> 2; matrix products, arithmetic and copies ran while one was open for 14% -> 6% of each run, Pallas kernels for 1% -> 3%
where the time goes in v4:
time: 97.1 us; the launch traced here: 96.7 us
  blocking collectives  47.5 us (49%)
  starting transfers between devices  15.3 us (16%)
  waiting for transfers between devices  15.1 us (16%)
  Pallas kernels  7.85 us (8%)
  matrix products  7.14 us (7%)
  between operations  2.24 us (2%)
  local copies, waits for them, and re-layouts  1.27 us (1%)
    all_gather x1, blocking collectives, gather(): lax.all_gather(both.reshape(2 * CAP, LIVE_DEV), 'z', axis=0, tiled=True)  47.5 us
    ppermute x3, waiting for transfers between devices, swap(): return lax.ppermute(value, axis, [(0, 1), (1, 0)])  13.1 us
    all_to_all x1, starting transfers between devices, shards(): lax.all_to_all(copies, CHIP, 0, 0, tiled=True).reshape(half, col_width)  9.48 us
    dot_general x3, matrix products, dot(): lax.dot_general(left, right, dims, preferred_element_type=jnp.float32)  7.14 us
    ppermute x3, starting transfers between devices, swap(): return lax.ppermute(value, axis, [(0, 1), (1, 0)])  5.86 us
    pallas_call x1, Pallas kernels, front(): pl.pallas_call(front_kernel, out_shape=(jax.ShapeDtypeStruct((chips, *red...  4.7 us
    pallas_call x1, Pallas kernels, ranks(): pl.pallas_call(ranks_kernel, out_shape=(grid, grid, jax.ShapeDtypeStruct(...  2.2 us
    all_to_all x1, waiting for transfers between devices, shards(): lax.all_to_all(copies, CHIP, 0, 0, tiled=True).reshape(half, col_width)  2.02 us
  transfers between devices with their start and end apart: 4, of which 2 were waited for; matrix products, arithmetic and copies ran while one was open for 6% of the time, Pallas kernels for 3%

profile of v4, /device:TPU:6, one launch (start us, length us, event | category | flops | bytes accessed | tf_op | source)
XLA Modules:
  0.0 96.7 jit_solution(88636830221049085)
XLA Ops:
  0.0 4.7 %front.1 = (bf16[8,128,1024]{2,1,0:T(8,128)(2,1)}, bf16[256,1024]{1,0:T(8,128)(2,1)}, bf16[256,1024]{1,0:T(8,128)(2,1)}, f32[1,1024]{1,0:T(1,128)S(1)}) custom-call(s32[16]{0:T(128)} %counts.1, s32[2,1024]{1,0:T(2,128)} %pivots.3, s32[512,1024]{1,0:T(8,128)} %rows.1, s32[128,1024]{1,0:T(8,128)} %bitcast.41), custom_call_target="tpu_custom_call" | custom-call | tf_op jit(solution)/shard_map/front/pallas_call | solution.py:168
  4.7 0.0 copy-start.6
  4.7 0.0 copy-start.1
  4.7 9.5 %all-to-all-start = ((bf16[8,128,1024]{2,1,0:T(8,128)(2,1)}), bf16[8,128,1024]{2,1,0:T(8,128)(2,1)S(1)}, u32[]{:S(2)}, u32[]{:S(2)}) async-start(bf16[8,128,1024]{2,1,0:T(8,128)(2,1)} %get-tuple-element.180), calls=%async_computation | async-start | bytes 4194304 | tf_op jit(solution)/shard_map/all_to_all | solution.py:232
  14.2 0.0 copy-done.6
  14.2 2.0 %collective-permute-start.1 = (bf16[256,1024]{1,0:T(8,128)(2,1)S(1)}, bf16[256,1024]{1,0:T(8,128)(2,1)S(1)}, u32[]{:S(2)}, u32[]{:S(2)}) collective-permute-start(bf16[256,1024]{1,0:T(8,128)(2,1)S(1)} %copy-done.6), channel_id=1, source_target_pairs={{0,32},{32,0},{1,33},{33,1},{2,34},{34,2},{3,35},{35,3},{4,36},{36... | collective-permute-start | bytes 1572872 | tf_op jit(solution)/shard_map/ppermute | solution.py:36
  16.3 0.0 copy-done.1
  16.3 2.2 %ranks.1 = (s32[2,8,128]{2,1,0:T(8,128)S(1)}, s32[2,8,128]{2,1,0:T(8,128)S(1)}, s32[1]{0:T(128)}) custom-call(s32[2,1024]{1,0:T(2,128)S(1)} %copy-done.1), custom_call_target="tpu_custom_call" | custom-call | flops 2000000000 | bytes 1000000 | tf_op jit(solution)/shard_map/ranks/pallas_call | solution.py:185
  18.5 0.0 collective-permute-done.1.incoming
  18.5 1.0 extract.1
  19.5 1.9 %collective-permute-start.2 = (s16[96,256]{1,0:T(8,128)(2,1)S(1)}, s16[96,256]{1,0:T(8,128)(2,1)S(1)}, u32[]{:S(2)}, u32[]{:S(2)}) collective-permute-start(s16[96,256]{1,0:T(8,128)(2,1)S(1)} %get-tuple-element.179), channel_id=1, source_target_pairs={{0,16},{16,0},{1,17},{17,1},{2,18},{18,2},{3,19},{19,3},{4,20},{20... | collective-permute-start | bytes 147464 | tf_op jit(solution)/shard_map/ppermute | solution.py:36
  23.5 13.1 %collective-permute-done.2 = s16[96,256]{1,0:T(8,128)(2,1)S(1)} collective-permute-done((s16[96,256]{1,0:T(8,128)(2,1)S(1)}, s16[96,256]{1,0:T(8,128)(2,1)S(1)}, u32[]{:S(2)}, u32[]{:S(2)}) %collective-permute-start.2) | collective-permute-done | bytes 49184 | tf_op jit(solution)/shard_map/ppermute | solution.py:36
  36.6 2.0 %all-to-all-done = bf16[8,128,1024]{2,1,0:T(8,128)(2,1)S(1)} async-done(((bf16[8,128,1024]{2,1,0:T(8,128)(2,1)}), bf16[8,128,1024]{2,1,0:T(8,128)(2,1)S(1)}, u32[]{:S(2)}, u32[]{:S(2)}) %all-to-all-start) | async-done | bytes 2097184 | tf_op jit(solution)/shard_map/all_to_all | solution.py:232
  38.6 1.9 %collective-permute-start.3 = (bf16[1024,1024]{1,0:T(8,128)(2,1)S(1)}, bf16[1024,1024]{1,0:T(8,128)(2,1)S(1)}, u32[]{:S(2)}, u32[]{:S(2)}) collective-permute-start(bf16[1024,1024]{1,0:T(8,128)(2,1)S(1)} %bitcast.35), channel_id=1, source_target_pairs={{0,32},{32,0},{1,33},{33,1},{2,34},{34,2},{3,35},{35,3},{4,36},{36... | collective-permute-start | bytes 6291464 | tf_op jit(solution)/shard_map/ppermute | solution.py:36
  40.5 47.5 %all-gather.2 = s16[3072,256]{1,0:T(8,128)(2,1)S(1)} all-gather(s16[192,256]{1,0:T(8,128)(2,1)S(1)} %bitcast.42), channel_id=1, replica_groups=mesh['yh'=2,'x'=4,'core'=2,'yl'=2,'z'=16] {'z'}, dimensions={0}, use_global_device_ids=true | all-gather | bytes 1671168 | tf_op jit(solution)/shard_map/all_gather | solution.py:226
  88.0 5.0 %fusion.15 = bf16[2048,256]{1,0:T(8,128)(2,1)S(1)} fusion(s32[2048]{0:T(1024)S(1)} %and_select_fusion, s16[3072,256]{1,0:T(8,128)(2,1)S(1)} %all-gather.2), kind=kOutput, calls=%fused_computation.29 | convolution fusion | flops 3228827648 | bytes 2629632 | tf_op jit(solution)/shard_map/dot_general | solution.py:40
  93.1 0.0 copy-start.5
  93.1 0.7 fusion.19
  93.8 0.0 collective-permute-done.3
  93.8 0.3 copy-done.5
  94.1 1.4 %fusion.17 = s32[256,1024]{1,0:T(8,128)S(1)} fusion(bf16[1024,1024]{1,0:T(8,128)(2,1)S(1)} %collective-permute-done.3, f32[256,1024]{1,0:T(8,128)S(1)} %fusion.19, bf16[256,1024]{1,0:T(8,128)(2,1)S(1)} %copy-done.5, bf16[2048,256]{1,0:T(8,128)(2,1)S(1)} %fusion.15), kind=kOutput, calls=%fused_computation.32 | convolution fusion | flops 543162368 | bytes 5242880 | tf_op jit(solution)/shard_map/dot_general | solution.py:40
  95.5 0.2 while.13
  95.7 0.0 copy-start.2
  95.7 1.0 copy-done.2
  (6 shorter events, 0.0 us)
Async XLA Ops:
  4.7 9.5 %copy-start.6 = (bf16[256,1024]{1,0:T(8,128)(2,1)S(1)}, bf16[256,1024]{1,0:T(8,128)(2,1)}, u32[]{:S(2)}) copy-start(bf16[256,1024]{1,0:T(8,128)(2,1)} %get-tuple-element.175) | copy-start | bytes 1572868
  4.7 11.6 %copy-start.1 = (s32[2,1024]{1,0:T(2,128)S(1)}, s32[2,1024]{1,0:T(2,128)}, u32[]{:S(2)}) copy-start(s32[2,1024]{1,0:T(2,128)} %pivots.3) | copy-start | bytes 24580
  4.7 33.8 %all-to-all-start = ((bf16[8,128,1024]{2,1,0:T(8,128)(2,1)}), bf16[8,128,1024]{2,1,0:T(8,128)(2,1)S(1)}, u32[]{:S(2)}, u32[]{:S(2)}) async-start(bf16[8,128,1024]{2,1,0:T(8,128)(2,1)} %get-tuple-element.180), calls=%async_computation | async-start | bytes 4194304 | tf_op jit(solution)/shard_map/all_to_all | solution.py:232
  14.2 4.3 %copy-start = (bf16[256,1024]{1,0:T(8,128)(2,1)S(1)}, bf16[256,1024]{1,0:T(8,128)(2,1)}, u32[]{:S(2)}) copy-start(bf16[256,1024]{1,0:T(8,128)(2,1)} %get-tuple-element.174.kept) | copy-start | bytes 1572868
  14.2 4.3 %collective-permute-start.1 = (bf16[256,1024]{1,0:T(8,128)(2,1)S(1)}, bf16[256,1024]{1,0:T(8,128)(2,1)S(1)}, u32[]{:S(2)}, u32[]{:S(2)}) collective-permute-start(bf16[256,1024]{1,0:T(8,128)(2,1)S(1)} %copy-done.6), channel_id=1, source_target_pairs={{0,32},{32,0},{1,33},{33,1},{2,34},{34,2},{3,35},{35,3},{4,36},{36... | collective-permute-start | bytes 1572872 | tf_op jit(solution)/shard_map/ppermute | solution.py:36
  19.5 17.1 %collective-permute-start.2 = (s16[96,256]{1,0:T(8,128)(2,1)S(1)}, s16[96,256]{1,0:T(8,128)(2,1)S(1)}, u32[]{:S(2)}, u32[]{:S(2)}) collective-permute-start(s16[96,256]{1,0:T(8,128)(2,1)S(1)} %get-tuple-element.179), channel_id=1, source_target_pairs={{0,16},{16,0},{1,17},{17,1},{2,18},{18,2},{3,19},{19,3},{4,20},{20... | collective-permute-start | bytes 147464 | tf_op jit(solution)/shard_map/ppermute | solution.py:36
  38.6 55.2 %collective-permute-start.3 = (bf16[1024,1024]{1,0:T(8,128)(2,1)S(1)}, bf16[1024,1024]{1,0:T(8,128)(2,1)S(1)}, u32[]{:S(2)}, u32[]{:S(2)}) collective-permute-start(bf16[1024,1024]{1,0:T(8,128)(2,1)S(1)} %bitcast.35), channel_id=1, source_target_pairs={{0,32},{32,0},{1,33},{33,1},{2,34},{34,2},{3,35},{35,3},{4,36},{36... | collective-permute-start | bytes 6291464 | tf_op jit(solution)/shard_map/ppermute | solution.py:36
  93.1 1.0 %copy-start.5 = (bf16[256,1024]{1,0:T(8,128)(2,1)S(1)}, bf16[256,1024]{1,0:T(8,128)(2,1)}, u32[]{:S(2)}) copy-start(bf16[256,1024]{1,0:T(8,128)(2,1)} %get-tuple-element.272) | copy-start | bytes 1572868
  93.8 1.7 %copy-start.3 = (bf16[1024,1024]{1,0:T(8,128)(2,1)}, bf16[1024,1024]{1,0:T(8,128)(2,1)S(1)}, u32[]{:S(2)}) copy-start(bf16[1024,1024]{1,0:T(8,128)(2,1)S(1)} %collective-permute-done.3) | copy-start | bytes 6291460
  95.7 1.0 %copy-start.2 = (s32[256,1024]{1,0:T(8,128)}, s32[256,1024]{1,0:T(8,128)S(1)}, u32[]{:S(2)}) copy-start(s32[256,1024]{1,0:T(8,128)S(1)} %get-tuple-element.305) | copy-start | bytes 3145732

commit v5 on v4

v5 whole, which is shorter than its diff:
```python
import jax
import jax.numpy as jnp
from jax import lax
from jax.experimental import pallas as pl
from jax.experimental.pallas import tpu as pltpu
from jax.sharding import Mesh, PartitionSpec as P


PANELS = 2
LIVE_DEV = 256
CAP = 96
LANES = 128

ROW = ("yh", "x", "core")
COL = ("yl", "z")
CHIP = ("yh", "x")

modulus = 241.0
half_modulus = 120.0

NN = (((1,), (0,)), ((), ()))
NT = (((1,), (1,)), ((), ()))
TN = (((0,), (0,)), ((), ()))


def centered(values):
    return values - modulus * (values > half_modulus).astype(values.dtype)


def remainder(values):
    rest = values - modulus * jnp.floor(values * (1.0 / modulus))
    rest = jnp.where(rest < 0.0, rest + modulus, rest)
    return jnp.where(rest >= modulus, rest - modulus, rest)


def swap(value, axis):
    return lax.ppermute(value, axis, [(0, 1), (1, 0)])


def dot(left, right, dims):
    return lax.dot_general(left, right, dims, preferred_element_type=jnp.float32)


def spread_row(grid):
    return jnp.concatenate([grid[i:i + 1] for i in range(grid.shape[0])], axis=1)


def one_hot(hits):
    return hits.astype(jnp.float32).astype(jnp.bfloat16)


def strictly_before(size):
    lower = lax.broadcasted_iota(jnp.int32, (size, size), 0)
    upper = lax.broadcasted_iota(jnp.int32, (size, size), 1)
    return one_hot(lower < upper)


def front_kernel(counts, pivots, rows, reducers, copies, placed, keep, send, slots, normed, done):
    width = rows.shape[1]
    capacity = rows.shape[0]
    groups = width // LANES
    core = lax.axis_index("core")
    upper = lax.axis_index("yl")
    depth = lax.axis_index("z")
    owner = (lax.axis_index("yh") * 4 + lax.axis_index("x")) * 2 + core
    start = (upper * 16 + depth) * width

    count = pivots.shape[1]
    lane_rows = lax.broadcasted_iota(jnp.int32, (LANES, count), 0)
    group_rows = lax.broadcasted_iota(jnp.int32, (2 * groups, count), 0)
    side = (lax.broadcasted_iota(jnp.int32, (1, count), 1) >> 6) & 1
    marks = jnp.zeros((2 * groups, LANES), jnp.float32)
    ahead = [jnp.zeros((1, 1), jnp.float32)] * 2
    for panel in range(PANELS):
        pivot = pivots[panel:panel + 1, :]
        place = pivot - start
        high = jnp.where((place >= 0) & (place < width), (place >> 7) + side * groups, -1)
        marks += dot(one_hot(group_rows == high), one_hot(lane_rows == (place & (LANES - 1))), NT)
        for half in range(2):
            first_block = ((pivot >> 10) == depth) & (side == half)
            ahead[half] += jnp.sum(first_block.astype(jnp.float32), axis=1, keepdims=True)
    flags = marks.astype(jnp.bfloat16)
    inside = dot(flags, strictly_before(LANES), NN)
    totals = dot(flags, jnp.ones((LANES, LANES), jnp.bfloat16), NN)
    group_ids = lax.broadcasted_iota(jnp.int32, (groups, LANES), 0)
    columns = []
    for half in range(2):
        part = slice(half * groups, (half + 1) * groups)
        place = inside[part] + jnp.where(upper == 0, 0.0, ahead[half])
        for group in range(groups - 1):
            place += jnp.where(group_ids > group, totals[half * groups + group:half * groups + group + 1], 0.0)
        columns.append(spread_row(jnp.where(marks[part] > 0.0, place, -1.0)))
        slots[half:half + 1, :] = columns[half]
    pivoted = marks[:groups] + marks[groups:]

    rows_dev = reducers.shape[0]
    part = rows_dev // PANELS
    own = pivots[:, pl.ds(pl.multiple_of((owner // 2) * LANES, LANES), LANES)].astype(jnp.float32)
    row_ids = lax.broadcasted_iota(jnp.int32, (rows_dev, LANES), 0)
    lane_ids = lax.broadcasted_iota(jnp.int32, (rows_dev, LANES), 1)
    chosen = jnp.where(row_ids < part, own[0:1], own[1:2])
    target = (row_ids & (part - 1)) + part * core
    own_pivot = jnp.sum(jnp.where(lane_ids == target, chosen, 0.0), axis=1, keepdims=True)
    base = start.astype(jnp.float32)
    for group in range(groups):
        cols = slice(group * LANES, (group + 1) * LANES)
        here = (lane_ids + group * LANES).astype(jnp.float32) + base
        entries = centered(reducers[:, cols].astype(jnp.float32))
        pivot_value = jnp.where(here == own_pivot, 1.0, 0.0)
        normed[:, cols] = jnp.where(pivoted[group:group + 1] > 0.0, pivot_value, entries).astype(jnp.bfloat16)
    writes = [pltpu.make_async_copy(normed, copies.at[chip], done.at[chip]) for chip in range(copies.shape[0])]
    for write in writes:
        write.start()

    first = counts[owner - core]
    mine = counts[owner]
    values = rows[...].astype(jnp.float32).astype(jnp.bfloat16)
    slot_ids = lax.broadcasted_iota(jnp.int32, (capacity, capacity), 1)
    places = lax.broadcasted_iota(jnp.int32, (capacity, capacity), 0)
    places = (places + LIVE_DEV * core) & (capacity - 1)
    pick = one_hot((slot_ids < mine) & (slot_ids == places - core * first))
    values = dot(pick, values, NN).astype(jnp.bfloat16)
    placed[...] = values

    want = lax.broadcasted_iota(jnp.int32, (CAP, width), 0).astype(jnp.float32)
    here = jnp.where(core == 0, columns[0], columns[1])
    there = jnp.where(core == 0, columns[1], columns[0])
    keep[...] = centered(dot(one_hot(here == want), values, NT)).astype(jnp.int32).astype(jnp.int16)
    other = centered(dot(one_hot(there == want), values, NT)).astype(jnp.int32).astype(jnp.int16)
    send[:, :LIVE_DEV] = other[:, LIVE_DEV:]
    send[:, LIVE_DEV:] = other[:, :LIVE_DEV]
    for write in writes:
        write.wait()


def ranks_kernel(pivots, ranks, slots, most):
    core = lax.axis_index("core")
    count = pivots.shape[1]
    chunks = 32768 // LANES
    lane_rows = lax.broadcasted_iota(jnp.int32, (LANES, count), 0)
    chunk_rows = lax.broadcasted_iota(jnp.int32, (chunks, count), 0)
    side = (lax.broadcasted_iota(jnp.int32, (1, count), 1) >> 6) & 1
    chunk_marks, lane_marks = [], []
    marks = [jnp.zeros((chunks, LANES), jnp.float32)] * 2
    for panel in range(PANELS):
        pivot = pivots[panel:panel + 1, :]
        chunk = pivot >> 7
        chunk_marks.append(one_hot(chunk_rows == chunk))
        lane_marks.append(lane_rows == (pivot & (LANES - 1)))
        lane_hot = one_hot(lane_marks[-1])
        for half in range(2):
            marks[half] += dot(one_hot(chunk_rows == jnp.where(side == half, chunk, -1)), lane_hot, NT)
    here = lax.broadcasted_iota(jnp.int32, (chunks, chunks), 0)
    other = lax.broadcasted_iota(jnp.int32, (chunks, chunks), 1)
    block, other_block = here >> 3, other >> 3
    earlier = one_hot(((block == other_block) & (other < here)) | (block == other_block + 16))
    tables = []
    for half in range(2):
        flags = marks[half].astype(jnp.bfloat16)
        totals = dot(flags, jnp.ones((LANES, LANES), jnp.bfloat16), NN).astype(jnp.bfloat16)
        tables.append(dot(flags, strictly_before(LANES), NN) + dot(earlier, totals, NN))
    most[0] = jnp.max(jnp.maximum(
        jnp.where(marks[0] > 0.0, tables[0], 0.0), jnp.where(marks[1] > 0.0, tables[1], 0.0)
    )).astype(jnp.int32)
    table = jnp.where(core == 0, tables[0], tables[1])
    high = jnp.floor(table * (1.0 / 128.0))
    low = (table - 128.0 * high).astype(jnp.bfloat16)
    high = high.astype(jnp.bfloat16)
    grids = []
    for panel in range(PANELS):
        found = 128.0 * dot(high, chunk_marks[panel], TN) + dot(low, chunk_marks[panel], TN)
        rank = jnp.sum(jnp.where(lane_marks[panel], found, 0.0), axis=0, keepdims=True).astype(jnp.int32)
        slot = ((pivots[panel:panel + 1, :] >> 10) & 15) * CAP + rank
        for value in (rank, slot):
            grids.append(jnp.concatenate([value[:, i * LANES:(i + 1) * LANES] for i in range(count // LANES)], axis=0))
    left = lax.broadcasted_iota(jnp.int32, grids[0].shape, 1) < LANES // 2
    for out, a, b in ((ranks, grids[0], grids[2]), (slots, grids[1], grids[3])):
        firsts = jnp.where(left, a, pltpu.roll(b, LANES // 2, axis=1))
        seconds = jnp.where(left, pltpu.roll(a, LANES // 2, axis=1), b)
        out[...] = jnp.where(core == 0, firsts, seconds)


VMEM = pl.BlockSpec(memory_space=pltpu.VMEM)
SMEM = pl.BlockSpec(memory_space=pltpu.SMEM)


def front(counts, pivots, rows, reducers, chips):
    capacity, width = rows.shape
    packed = jax.ShapeDtypeStruct((CAP, capacity), jnp.int16)
    return pl.pallas_call(
        front_kernel,
        out_shape=(
            jax.ShapeDtypeStruct((chips, *reducers.shape), jnp.bfloat16),
            jax.ShapeDtypeStruct((capacity, width), jnp.bfloat16),
            packed,
            packed,
            jax.ShapeDtypeStruct((2, width), jnp.float32),
        ),
        in_specs=[SMEM, VMEM, VMEM, VMEM],
        out_specs=(pl.BlockSpec(memory_space=pl.ANY), VMEM, VMEM, VMEM, VMEM),
        scratch_shapes=[pltpu.VMEM(reducers.shape, jnp.bfloat16), pltpu.SemaphoreType.DMA((chips,))],
        name="front",
    )(counts, pivots, rows, reducers)


def ranks(pivots):
    grid = jax.ShapeDtypeStruct((pivots.shape[1] // LANES, LANES), jnp.int32)
    return pl.pallas_call(
        ranks_kernel,
        out_shape=(grid, grid, jax.ShapeDtypeStruct((1,), jnp.int32)),
        in_specs=[VMEM],
        out_specs=(VMEM, VMEM, SMEM),
        name="ranks",
        compiler_params=pltpu.CompilerParams(vmem_limit_bytes=16 << 20),
        cost_estimate=pl.CostEstimate(flops=2_000_000_000, bytes_accessed=1_000_000, transcendentals=0),
    )(pivots)


def shards(pair_rows, reducers, pivots, counts):
    core = lax.axis_index("core")
    chips = lax.axis_size(CHIP)
    col_width = pair_rows.shape[1]
    rows_dev = PANELS * reducers.shape[1]
    half = chips * rows_dev
    copies, placed, keep, send, columns = front(counts, pivots, pair_rows, reducers.reshape(rows_dev, col_width), chips)
    my_rank, my_slot, most = ranks(pivots)
    my_rank, my_slot = my_rank.reshape(-1), my_slot.reshape(-1)
    rounds = most[0] // CAP + 1

    def gather(keep, send, base):
        both = keep + swap(send, "core")
        both = both + swap(both, "yl")
        spread = lax.all_gather(both, "z", axis=0, tiled=True)
        here = jnp.where((my_rank >= base) & (my_rank < base + CAP), my_slot - base, -1)
        table = (here[:, None] == lax.iota(jnp.int32, spread.shape[0])[None, :]).astype(jnp.bfloat16)
        factors = dot(table, spread.astype(jnp.bfloat16), NN)
        return factors.astype(jnp.bfloat16)

    panel = lax.all_to_all(copies, CHIP, 0, 0, tiled=True).reshape(half, col_width)
    factors = gather(keep, send, 0)

    def another(state):
        step, factors = state
        base = step * CAP
        want = (lax.iota(jnp.int32, CAP) + base).astype(jnp.float32)
        more = [
            centered(dot((columns[side] == want[:, None]).astype(jnp.bfloat16), placed, NT)).astype(jnp.int16)
            for side in range(2)
        ]
        keep = jnp.where(core == 0, more[0], more[1])
        send = jnp.roll(jnp.where(core == 0, more[1], more[0]), LIVE_DEV, axis=1)
        return step + 1, factors + gather(keep, send, base)

    _, factors = lax.while_loop(lambda state: state[0] < rounds, another, (jnp.int32(1), factors))

    def reduced(start):
        rows = slice(start, start + LIVE_DEV)
        return remainder(placed[rows].astype(jnp.float32) - dot(factors[:, rows], panel, TN))

    incoming = swap(reduced(LIVE_DEV).astype(jnp.bfloat16), "core")
    own = lax.optimization_barrier(reduced(0))
    result = own + incoming.astype(jnp.float32)
    return jnp.where(result >= modulus, result - modulus, result).astype(jnp.int32)


def solution(mesh):
    fine = Mesh(mesh.devices.reshape(2, 4, 2, 2, 16), (*ROW, *COL))
    return jax.shard_map(
        shards,
        mesh=fine,
        in_specs=(P(ROW, COL), P(None, ROW, COL), P(), P()),
        out_specs=P(ROW, COL),
        check_vma=False,
    )
```

time: 97.1 us -> 94.7 us (0.975)
  the two profiles are of different devices: /device:TPU:6 before, /device:TPU:1 now
where the time goes in v5:
time: 94.7 us; the launch traced here: 94.3 us
  blocking collectives  39.2 us (41%)
  starting transfers between devices  22.9 us (24%)
  waiting for transfers between devices  16 us (17%)
  Pallas kernels  6.69 us (7%)
  matrix products  5.97 us (6%)
  between operations  2.22 us (2%)
  other arithmetic  1.27 us (1%)
    all_gather x1, blocking collectives, gather(): spread = lax.all_gather(both, 'z', axis=0, tiled=True)  39.2 us
    ppermute x3, waiting for transfers between devices, swap(): return lax.ppermute(value, axis, [(0, 1), (1, 0)])  16 us
    ppermute x3, starting transfers between devices, swap(): return lax.ppermute(value, axis, [(0, 1), (1, 0)])  15.3 us
    all_to_all x1, starting transfers between devices, shards(): lax.all_to_all(copies, CHIP, 0, 0, tiled=True).reshape(half, col_width)  7.61 us
    dot_general x3, matrix products, dot(): lax.dot_general(left, right, dims, preferred_element_type=jnp.float32)  5.97 us
    pallas_call x1, Pallas kernels, front(): pl.pallas_call(front_kernel, out_shape=(jax.ShapeDtypeStruct((chips, *red...  4.4 us
    pallas_call x1, Pallas kernels, ranks(): pl.pallas_call(ranks_kernel, out_shape=(grid, grid, jax.ShapeDtypeStruct(...  2.29 us
  transfers between devices with their start and end apart: 4, of which 2 were waited for; matrix products, arithmetic and copies ran while one was open for 4% of the time, Pallas kernels for 2%

profile of v5, /device:TPU:1, one launch (start us, length us, event | category | flops | bytes accessed | tf_op | source)
XLA Modules:
  0.0 94.3 jit_solution(9613523708959958694)
XLA Ops:
  0.0 4.4 %front.1 = (bf16[8,128,1024]{2,1,0:T(8,128)(2,1)}, bf16[512,1024]{1,0:T(8,128)(2,1)S(1)}, s16[96,512]{1,0:T(8,128)(2,1)}, s16[96,512]{1,0:T(8,128)(2,1)}, f32[2,1024]{1,0:T(2,128)S(1)}) custom-call(s32[16]{0:T(128)} %counts.1, s32[2,1024]{1,0:T(2,128)} %pivots.3, s32[512,1024]{1,0:T(8,128)} %rows.1, s32[128,1024]{1,0:T(8,128)} %bitcast.24), custom_call_target="tpu_custom_call" | custom-call | tf_op jit(solution)/shard_map/front/pallas_call | solution.py:190
  4.4 0.0 copy-start.2
  4.4 0.0 copy-start
  4.4 7.6 %all-to-all-start = ((bf16[8,128,1024]{2,1,0:T(8,128)(2,1)}), bf16[8,128,1024]{2,1,0:T(8,128)(2,1)S(1)}, u32[]{:S(2)}, u32[]{:S(2)}) async-start(bf16[8,128,1024]{2,1,0:T(8,128)(2,1)} %get-tuple-element.118), calls=%async_computation | async-start | bytes 4194304 | tf_op jit(solution)/shard_map/all_to_all | solution.py:239
  12.0 0.0 copy-done.2
  12.0 0.0 copy-start.1
  12.1 5.0 %collective-permute-start.2 = (s16[96,512]{1,0:T(8,128)(2,1)S(1)}, s16[96,512]{1,0:T(8,128)(2,1)S(1)}, u32[]{:S(2)}, u32[]{:S(2)}) collective-permute-start(s16[96,512]{1,0:T(8,128)(2,1)S(1)} %copy-done.2), channel_id=1, source_target_pairs={{0,32},{32,0},{1,33},{33,1},{2,34},{34,2},{3,35},{35,3},{4,36},{36... | collective-permute-start | bytes 294920 | tf_op jit(solution)/shard_map/ppermute | solution.py:37
  17.1 0.0 copy-done
  17.1 2.3 %ranks.1 = (s32[8,128]{1,0:T(8,128)S(1)}, s32[8,128]{1,0:T(8,128)S(1)}, s32[1]{0:T(128)}) custom-call(s32[2,1024]{1,0:T(2,128)S(1)} %copy-done), custom_call_target="tpu_custom_call" | custom-call | flops 2000000000 | bytes 1000000 | tf_op jit(solution)/shard_map/ranks/pallas_call | solution.py:208
  19.4 0.0 collective-permute-done.2
  19.4 0.0 copy-done.1
  19.5 1.9 %collective-permute-start.3 = (s16[96,512]{1,0:T(8,128)(2,1)S(1)}, s16[96,512]{1,0:T(8,128)(2,1)S(1)}, u32[]{:S(2)}, u32[]{:S(2)}) collective-permute-start(s16[96,512]{1,0:T(8,128)(2,1)S(1)} %add.59), channel_id=1, source_target_pairs={{0,16},{16,0},{1,17},{17,1},{2,18},{18,2},{3,19},{19,3},{4,20},{20... | collective-permute-start | bytes 294920 | tf_op jit(solution)/shard_map/ppermute | solution.py:37
  23.5 15.5 %collective-permute-done.3 = s16[96,512]{1,0:T(8,128)(2,1)S(1)} collective-permute-done((s16[96,512]{1,0:T(8,128)(2,1)S(1)}, s16[96,512]{1,0:T(8,128)(2,1)S(1)}, u32[]{:S(2)}, u32[]{:S(2)}) %collective-permute-start.3) | collective-permute-done | bytes 98336 | tf_op jit(solution)/shard_map/ppermute | solution.py:37
  39.0 39.2 %all-gather.2 = s16[1536,512]{1,0:T(8,128)(2,1)S(1)} all-gather(s16[96,512]{1,0:T(8,128)(2,1)S(1)} %add.60), channel_id=1, replica_groups=mesh['yh'=2,'x'=4,'core'=2,'yl'=2,'z'=16] {'z'}, dimensions={0}, use_global_device_ids=true | all-gather | bytes 1671168 | tf_op jit(solution)/shard_map/all_gather | solution.py:233
  78.3 2.8 %fusion.24 = bf16[1024,512]{1,0:T(8,128)(2,1)} fusion(s16[1536,512]{1,0:T(8,128)(2,1)S(1)} %all-gather.2, s32[1024]{0:T(1024)S(1)} %and_select_fusion), kind=kOutput, calls=%fused_computation.30 | convolution fusion | flops 1613496320 | bytes 2625536 | tf_op jit(solution)/shard_map/dot_general | solution.py:41
  81.1 0.0 all-to-all-done
  81.1 0.0 copy-start.3
  81.1 2.1 %fusion.27 = bf16[256,1024]{1,0:T(8,128)(2,1)S(1)} fusion(bf16[1024,1024]{1,0:T(8,128)(2,1)S(1)} %bitcast.22, bf16[1024,512]{1,0:T(8,128)(2,1)} %get-tuple-element.117, bf16[512,1024]{1,0:T(8,128)(2,1)S(1)} %get-tuple-element.233), kind=kOutput, calls=%fused_computation.33 | convolution fusion | flops 540278784 | bytes 3670016 | tf_op jit(solution)/shard_map/dot_general | solution.py:41
  83.2 8.3 %collective-permute-start.4 = (bf16[256,1024]{1,0:T(8,128)(2,1)S(1)}, bf16[256,1024]{1,0:T(8,128)(2,1)S(1)}, u32[]{:S(2)}, u32[]{:S(2)}) collective-permute-start(bf16[256,1024]{1,0:T(8,128)(2,1)S(1)} %fusion.27), channel_id=1, source_target_pairs={{0,32},{32,0},{1,33},{33,1},{2,34},{34,2},{3,35},{35,3},{4,36},{36... | collective-permute-start | bytes 1572872 | tf_op jit(solution)/shard_map/ppermute | solution.py:37
  91.6 0.0 copy-done.3
  91.6 1.0 %compare_select_fusion.3 = f32[256,1024]{1,0:T(8,128)S(1)} fusion(bf16[1024,1024]{1,0:T(8,128)(2,1)S(1)} %bitcast.23, bf16[1024,512]{1,0:T(8,128)(2,1)S(1)} %copy-done.3, bf16[512,1024]{1,0:T(8,128)(2,1)S(1)} %get-tuple-element.233), kind=kOutput, calls=%fused_computation.27 | convolution fusion | flops 540016640 | bytes 4194304 | tf_op jit(solution)/shard_map/dot_general | solution.py:41
  92.6 0.5 collective-permute-done.4
  93.1 1.2 %fusion.28 = s32[256,1024]{1,0:T(8,128)} fusion(f32[256,1024]{1,0:T(8,128)S(1)} %compare_select_fusion.3, bf16[256,1024]{1,0:T(8,128)(2,1)S(1)} %collective-permute-done.4), kind=kLoop, calls=%fused_computation.34 | loop fusion | flops 1572864 | bytes 2621440 | tf_op jit(solution)/shard_map/convert_element_type | solution.py:263
  (4 shorter events, 0.1 us)
Async XLA Ops:
  4.4 7.6 %copy-start.2 = (s16[96,512]{1,0:T(8,128)(2,1)S(1)}, s16[96,512]{1,0:T(8,128)(2,1)}, u32[]{:S(2)}) copy-start(s16[96,512]{1,0:T(8,128)(2,1)} %get-tuple-element.114) | copy-start | bytes 294916
  4.4 12.7 %copy-start = (s32[2,1024]{1,0:T(2,128)S(1)}, s32[2,1024]{1,0:T(2,128)}, u32[]{:S(2)}) copy-start(s32[2,1024]{1,0:T(2,128)} %pivots.3) | copy-start | bytes 24580
  4.4 76.7 %all-to-all-start = ((bf16[8,128,1024]{2,1,0:T(8,128)(2,1)}), bf16[8,128,1024]{2,1,0:T(8,128)(2,1)S(1)}, u32[]{:S(2)}, u32[]{:S(2)}) async-start(bf16[8,128,1024]{2,1,0:T(8,128)(2,1)} %get-tuple-element.118), calls=%async_computation | async-start | bytes 4194304 | tf_op jit(solution)/shard_map/all_to_all | solution.py:239
  12.0 7.4 %copy-start.1 = (s16[96,512]{1,0:T(8,128)(2,1)S(1)}, s16[96,512]{1,0:T(8,128)(2,1)}, u32[]{:S(2)}) copy-start(s16[96,512]{1,0:T(8,128)(2,1)} %get-tuple-element.113) | copy-start | bytes 294916
  12.1 7.3 %collective-permute-start.2 = (s16[96,512]{1,0:T(8,128)(2,1)S(1)}, s16[96,512]{1,0:T(8,128)(2,1)S(1)}, u32[]{:S(2)}, u32[]{:S(2)}) collective-permute-start(s16[96,512]{1,0:T(8,128)(2,1)S(1)} %copy-done.2), channel_id=1, source_target_pairs={{0,32},{32,0},{1,33},{33,1},{2,34},{34,2},{3,35},{35,3},{4,36},{36... | collective-permute-start | bytes 294920 | tf_op jit(solution)/shard_map/ppermute | solution.py:37
  19.5 19.6 %collective-permute-start.3 = (s16[96,512]{1,0:T(8,128)(2,1)S(1)}, s16[96,512]{1,0:T(8,128)(2,1)S(1)}, u32[]{:S(2)}, u32[]{:S(2)}) collective-permute-start(s16[96,512]{1,0:T(8,128)(2,1)S(1)} %add.59), channel_id=1, source_target_pairs={{0,16},{16,0},{1,17},{17,1},{2,18},{18,2},{3,19},{19,3},{4,20},{20... | collective-permute-start | bytes 294920 | tf_op jit(solution)/shard_map/ppermute | solution.py:37
  81.1 10.5 %copy-start.3 = (bf16[1024,512]{1,0:T(8,128)(2,1)S(1)}, bf16[1024,512]{1,0:T(8,128)(2,1)}, u32[]{:S(2)}) copy-start(bf16[1024,512]{1,0:T(8,128)(2,1)} %get-tuple-element.117) | copy-start | bytes 3145732
  83.2 9.9 %collective-permute-start.4 = (bf16[256,1024]{1,0:T(8,128)(2,1)S(1)}, bf16[256,1024]{1,0:T(8,128)(2,1)S(1)}, u32[]{:S(2)}, u32[]{:S(2)}) collective-permute-start(bf16[256,1024]{1,0:T(8,128)(2,1)S(1)} %fusion.27), channel_id=1, source_target_pairs={{0,32},{32,0},{1,33},{33,1},{2,34},{34,2},{3,35},{35,3},{4,36},{36... | collective-permute-start | bytes 1572872 | tf_op jit(solution)/shard_map/ppermute | solution.py:37

commit v6 on v5

v6 whole, which is shorter than its diff:
```python
import functools

import jax
import jax.numpy as jnp
from jax import lax
from jax.experimental import pallas as pl
from jax.experimental.pallas import tpu as pltpu
from jax.sharding import Mesh, PartitionSpec as P


PANELS = 2
LIVE_DEV = 256
CAP = 96
LANES = 128

ROW = ("yh", "x", "core")
COL = ("yl", "z")
CHIP = ("yh", "x")

modulus = 241.0
half_modulus = 120.0

NN = (((1,), (0,)), ((), ()))
NT = (((1,), (1,)), ((), ()))
TN = (((0,), (0,)), ((), ()))


def centered(values):
    return values - modulus * (values > half_modulus).astype(values.dtype)


def remainder(values):
    rest = values - modulus * jnp.floor(values * (1.0 / modulus))
    rest = jnp.where(rest < 0.0, rest + modulus, rest)
    return jnp.where(rest >= modulus, rest - modulus, rest)


def swap(value, axis):
    return lax.ppermute(value, axis, [(0, 1), (1, 0)])


def dot(left, right, dims):
    return lax.dot_general(left, right, dims, preferred_element_type=jnp.float32)


def spread_row(grid):
    return jnp.concatenate([grid[i:i + 1] for i in range(grid.shape[0])], axis=1)


def one_hot(hits):
    return hits.astype(jnp.float32).astype(jnp.bfloat16)


def strictly_before(size):
    lower = lax.broadcasted_iota(jnp.int32, (size, size), 0)
    upper = lax.broadcasted_iota(jnp.int32, (size, size), 1)
    return one_hot(lower < upper)


def front_kernel(
    counts, pivots, rows_in, reducers_in, copies, placed, keep, send, slots, rows, reducers, normed, done, come
):
    reads = [
        pltpu.make_async_copy(reducers_in, reducers, come.at[0]),
        pltpu.make_async_copy(rows_in, rows, come.at[1]),
    ]
    for read in reads:
        read.start()
    width = rows.shape[1]
    capacity = rows.shape[0]
    groups = width // LANES
    core = lax.axis_index("core")
    upper = lax.axis_index("yl")
    depth = lax.axis_index("z")
    owner = (lax.axis_index("yh") * 4 + lax.axis_index("x")) * 2 + core
    start = (upper * 16 + depth) * width

    count = pivots.shape[1]
    lane_rows = lax.broadcasted_iota(jnp.int32, (LANES, count), 0)
    group_rows = lax.broadcasted_iota(jnp.int32, (2 * groups, count), 0)
    side = (lax.broadcasted_iota(jnp.int32, (1, count), 1) >> 6) & 1
    marks = jnp.zeros((2 * groups, LANES), jnp.float32)
    ahead = [jnp.zeros((1, 1), jnp.float32)] * 2
    for panel in range(PANELS):
        pivot = pivots[panel:panel + 1, :]
        place = pivot - start
        high = jnp.where((place >= 0) & (place < width), (place >> 7) + side * groups, -1)
        marks += dot(one_hot(group_rows == high), one_hot(lane_rows == (place & (LANES - 1))), NT)
        for half in range(2):
            first_block = ((pivot >> 10) == depth) & (side == half)
            ahead[half] += jnp.sum(first_block.astype(jnp.float32), axis=1, keepdims=True)
    flags = marks.astype(jnp.bfloat16)
    inside = dot(flags, strictly_before(LANES), NN)
    totals = dot(flags, jnp.ones((LANES, LANES), jnp.bfloat16), NN)
    group_ids = lax.broadcasted_iota(jnp.int32, (groups, LANES), 0)
    columns = []
    for half in range(2):
        part = slice(half * groups, (half + 1) * groups)
        place = inside[part] + jnp.where(upper == 0, 0.0, ahead[half])
        for group in range(groups - 1):
            place += jnp.where(group_ids > group, totals[half * groups + group:half * groups + group + 1], 0.0)
        columns.append(spread_row(jnp.where(marks[part] > 0.0, place, -1.0)))
    pivoted = marks[:groups] + marks[groups:]

    rows_dev = reducers.shape[0]
    part = rows_dev // PANELS
    own = pivots[:, pl.ds(pl.multiple_of((owner // 2) * LANES, LANES), LANES)].astype(jnp.float32)
    row_ids = lax.broadcasted_iota(jnp.int32, (rows_dev, LANES), 0)
    lane_ids = lax.broadcasted_iota(jnp.int32, (rows_dev, LANES), 1)
    chosen = jnp.where(row_ids < part, own[0:1], own[1:2])
    target = (row_ids & (part - 1)) + part * core
    own_pivot = jnp.sum(jnp.where(lane_ids == target, chosen, 0.0), axis=1, keepdims=True)
    base = start.astype(jnp.float32)
    reads[0].wait()
    for group in range(groups):
        cols = slice(group * LANES, (group + 1) * LANES)
        here = (lane_ids + group * LANES).astype(jnp.float32) + base
        entries = centered(reducers[:, cols].astype(jnp.float32))
        pivot_value = jnp.where(here == own_pivot, 1.0, 0.0)
        normed[:, cols] = jnp.where(pivoted[group:group + 1] > 0.0, pivot_value, entries).astype(jnp.bfloat16)
    writes = [pltpu.make_async_copy(normed, copies.at[chip], done.at[chip]) for chip in range(copies.shape[0])]
    for write in writes:
        write.start()

    first = counts[owner - core]
    mine = counts[owner]
    slot_ids = lax.broadcasted_iota(jnp.int32, (capacity, capacity), 1)
    places = lax.broadcasted_iota(jnp.int32, (capacity, capacity), 0)
    places = (places + LIVE_DEV * core) & (capacity - 1)
    pick = one_hot((slot_ids < mine) & (slot_ids == places - core * first))
    reads[1].wait()
    values = rows[...].astype(jnp.float32).astype(jnp.bfloat16)
    values = dot(pick, values, NN).astype(jnp.bfloat16)
    placed[...] = values

    want = lax.broadcasted_iota(jnp.int32, (CAP, width), 0).astype(jnp.float32)
    here = jnp.where(core == 0, columns[0], columns[1])
    there = jnp.where(core == 0, columns[1], columns[0])
    slots[0:1, :], slots[1:2, :] = here, there
    keep[...] = centered(dot(one_hot(here == want), values, NT)).astype(jnp.int32).astype(jnp.int16)
    other = centered(dot(one_hot(there == want), values, NT)).astype(jnp.int32).astype(jnp.int16)
    send[:, :LIVE_DEV] = other[:, LIVE_DEV:]
    send[:, LIVE_DEV:] = other[:, :LIVE_DEV]
    for write in writes:
        write.wait()


def ranks_kernel(pivots, ranks, slots, firsts, extra):
    core = lax.axis_index("core")
    count = pivots.shape[1]
    chunks = 32768 // LANES
    both = 2 * LANES
    lane_rows = lax.broadcasted_iota(jnp.int32, (both, count), 0)
    chunk_rows = lax.broadcasted_iota(jnp.int32, (chunks, count), 0)
    side = (lax.broadcasted_iota(jnp.int32, (1, count), 1) >> 6) & 1
    chunk_marks = []
    marks = jnp.zeros((chunks, both), jnp.float32)
    for panel in range(PANELS):
        pivot = pivots[panel:panel + 1, :]
        chunk_marks.append(one_hot(chunk_rows == (pivot >> 7)))
        marks += dot(chunk_marks[-1], one_hot(lane_rows == ((pivot & (LANES - 1)) + side * LANES)), NT)
    flags = marks.astype(jnp.bfloat16)
    here = lax.broadcasted_iota(jnp.int32, (chunks, chunks), 0)
    other = lax.broadcasted_iota(jnp.int32, (chunks, chunks), 1)
    block, other_block = here >> 3, other >> 3
    earlier = one_hot(((block == other_block) & (other < here)) | (block == other_block + 16))
    same_side = (here >> 7) == (other >> 7)
    totals = dot(flags, one_hot(same_side), NN).astype(jnp.bfloat16)
    table = dot(flags, one_hot(same_side & (here < other)), NN) + dot(earlier, totals, NN)
    extra[0] = jnp.max(jnp.where(marks > 0.0, table, 0.0)).astype(jnp.int32) // CAP
    table = jnp.where(core == 0, table[:, :LANES], table[:, LANES:])
    high = jnp.floor(table * (1.0 / 128.0))
    parts = jnp.concatenate([high, table - 128.0 * high], axis=1).astype(jnp.bfloat16)
    grids = []
    for panel in range(PANELS):
        pivot = pivots[panel:panel + 1, :]
        found = dot(parts, chunk_marks[panel], TN)
        found = 128.0 * found[:LANES] + found[LANES:]
        rank = jnp.where(lane_rows[:LANES] == (pivot & (LANES - 1)), found, 0.0)
        rank = jnp.sum(rank, axis=0, keepdims=True).astype(jnp.int32)
        for value in (rank, ((pivot >> 10) & 15) * CAP + rank):
            grids.append(jnp.concatenate([value[:, i * LANES:(i + 1) * LANES] for i in range(count // LANES)], axis=0))
    left = lax.broadcasted_iota(jnp.int32, grids[0].shape, 1) < LANES // 2
    picked = []
    for a, b in ((grids[0], grids[2]), (grids[1], grids[3])):
        lows = jnp.where(left, a, pltpu.roll(b, LANES // 2, axis=1))
        highs = jnp.where(left, pltpu.roll(a, LANES // 2, axis=1), b)
        picked.append(jnp.where(core == 0, lows, highs))
    ranks[...], slots[...] = picked
    firsts[...] = jnp.where(picked[0] < CAP, picked[1], -1)


def reduce_kernel(first_row, spread, where, placed, panel_in, out, panel, come):
    depth = 2 * LANES
    blocks = panel.shape[0] // depth
    reads = []
    for block in range(blocks):
        part = pl.ds(block * depth, depth)
        reads.append(pltpu.make_async_copy(panel_in.at[part], panel.at[part], come.at[block]))
        reads[block].start()
    rows = slice(first_row, first_row + LIVE_DEV)
    slot_count = spread.shape[0]
    packed = jnp.transpose(spread[:, rows].astype(jnp.int32).astype(jnp.float32)).astype(jnp.bfloat16)
    slot_rows = lax.broadcasted_iota(jnp.int32, (slot_count, depth), 0)
    total = jnp.zeros(out.shape, jnp.float32)
    for block in range(blocks):
        here = spread_row(where[2 * block:2 * block + 2, :])
        factors = dot(packed, one_hot(slot_rows == here), NN).astype(jnp.bfloat16)
        reads[block].wait()
        total += dot(factors, panel[block * depth:(block + 1) * depth, :], NN)
    out[...] = remainder(placed[rows, :].astype(jnp.float32) - total).astype(jnp.bfloat16)


def combine_kernel(own, incoming, out, result, done):
    step = LIVE_DEV // done.shape[0]
    writes = []
    for part in range(done.shape[0]):
        rows = slice(part * step, (part + 1) * step)
        total = own[rows, :].astype(jnp.float32) + incoming[rows, :].astype(jnp.float32)
        result[rows, :] = jnp.where(total >= modulus, total - modulus, total).astype(jnp.int32)
        write = pltpu.make_async_copy(result.at[pl.ds(part * step, step)], out.at[pl.ds(part * step, step)], done.at[part])
        write.start()
        writes.append(write)
    for write in writes:
        write.wait()


VMEM = pl.BlockSpec(memory_space=pltpu.VMEM)
SMEM = pl.BlockSpec(memory_space=pltpu.SMEM)
ANY = pl.BlockSpec(memory_space=pl.ANY)


def front(counts, pivots, rows, reducers, chips):
    capacity, width = rows.shape
    packed = jax.ShapeDtypeStruct((CAP, capacity), jnp.int16)
    return pl.pallas_call(
        front_kernel,
        out_shape=(
            jax.ShapeDtypeStruct((chips, *reducers.shape), jnp.bfloat16),
            jax.ShapeDtypeStruct((capacity, width), jnp.bfloat16),
            packed,
            packed,
            jax.ShapeDtypeStruct((2, width), jnp.float32),
        ),
        in_specs=[SMEM, VMEM, ANY, ANY],
        out_specs=(ANY, VMEM, VMEM, VMEM, VMEM),
        scratch_shapes=[
            pltpu.VMEM(rows.shape, jnp.int32),
            pltpu.VMEM(reducers.shape, jnp.int32),
            pltpu.VMEM(reducers.shape, jnp.bfloat16),
            pltpu.SemaphoreType.DMA((chips,)),
            pltpu.SemaphoreType.DMA((2,)),
        ],
        name="front",
    )(counts, pivots, rows, reducers)


def ranks(pivots):
    grid = jax.ShapeDtypeStruct((pivots.shape[1] // LANES, LANES), jnp.int32)
    return pl.pallas_call(
        ranks_kernel,
        out_shape=(grid, grid, grid, jax.ShapeDtypeStruct((1,), jnp.int32)),
        in_specs=[VMEM],
        out_specs=(VMEM, VMEM, VMEM, SMEM),
        name="ranks",
        compiler_params=pltpu.CompilerParams(vmem_limit_bytes=16 << 20),
        cost_estimate=pl.CostEstimate(flops=2_000_000_000, bytes_accessed=1_000_000, transcendentals=0),
    )(pivots)


def reduced(first_row, spread, where, placed, panel):
    width = panel.shape[1]
    return pl.pallas_call(
        functools.partial(reduce_kernel, first_row),
        out_shape=jax.ShapeDtypeStruct((LIVE_DEV, width), jnp.bfloat16),
        in_specs=[VMEM, VMEM, VMEM, ANY],
        out_specs=VMEM,
        scratch_shapes=[pltpu.VMEM(panel.shape, jnp.bfloat16), pltpu.SemaphoreType.DMA((panel.shape[0] // (2 * LANES),))],
        compiler_params=pltpu.CompilerParams(vmem_limit_bytes=24 << 20),
        cost_estimate=pl.CostEstimate(flops=1_500_000_000, bytes_accessed=5_000_000, transcendentals=0),
    )(spread, where, placed, panel)


def combine(own, incoming):
    return pl.pallas_call(
        combine_kernel,
        out_shape=jax.ShapeDtypeStruct(own.shape, jnp.int32),
        in_specs=[VMEM] * 2,
        out_specs=pl.BlockSpec(memory_space=pltpu.HBM),
        scratch_shapes=[pltpu.VMEM(own.shape, jnp.int32), pltpu.SemaphoreType.DMA((4,))],
        name="combine",
        compiler_params=pltpu.CompilerParams(vmem_limit_bytes=8 << 20),
    )(own, incoming)


def shards(pair_rows, reducers, pivots, counts):
    chips = lax.axis_size(CHIP)
    col_width = pair_rows.shape[1]
    rows_dev = PANELS * reducers.shape[1]
    half = chips * rows_dev
    copies, placed, keep, send, columns = front(counts, pivots, pair_rows, reducers.reshape(rows_dev, col_width), chips)
    my_rank, my_slot, firsts, extra = ranks(pivots)

    def gather(keep, send):
        both = keep + swap(send, "core")
        both = both + swap(both, "yl")
        return lax.all_gather(both, "z", axis=0, tiled=True)

    panel = lax.all_to_all(copies, CHIP, 0, 0, tiled=True).reshape(half, col_width)
    spread = gather(keep, send)
    incoming = reduced(LIVE_DEV, spread, firsts, placed, panel)
    incoming = swap(incoming, "core")
    own = reduced(0, spread, firsts, placed, panel)
    first = combine(own, incoming)

    def another(state):
        step, result = state
        base = step * CAP
        want = (lax.iota(jnp.int32, CAP) + base).astype(jnp.float32)
        keep, send = [
            centered(dot((columns[side] == want[:, None]).astype(jnp.bfloat16), placed, NT)).astype(jnp.int16)
            for side in range(2)
        ]
        spread = gather(keep, jnp.roll(send, LIVE_DEV, axis=1)).astype(jnp.bfloat16)
        where = jnp.where((my_rank >= base) & (my_rank < base + CAP), my_slot - base, -1).reshape(-1, 1)
        table = (where == lax.iota(jnp.int32, spread.shape[0])[None, :]).astype(jnp.bfloat16)
        products = remainder(dot(dot(table, spread, NN).astype(jnp.bfloat16), panel, TN))
        incoming = swap(products[LIVE_DEV:].astype(jnp.bfloat16), "core").astype(jnp.float32)
        result = result.astype(jnp.float32) - products[:LIVE_DEV] - incoming
        return step - 1, remainder(result).astype(jnp.int32)

    _, result = lax.while_loop(lambda state: state[0] > 0, another, (extra[0], first))
    return result


def solution(mesh):
    fine = Mesh(mesh.devices.reshape(2, 4, 2, 2, 16), (*ROW, *COL))
    return jax.shard_map(
        shards,
        mesh=fine,
        in_specs=(P(ROW, COL), P(None, ROW, COL), P(), P()),
        out_specs=P(ROW, COL),
        check_vma=False,
    )
```

time: 94.7 us -> 96.3 us (1.017)
  the two profiles are of different devices: /device:TPU:1 before, /device:TPU:3 now
where the time goes in v6:
time: 96.3 us; the launch traced here: 95.9 us
  blocking collectives  37.5 us (39%)
  starting transfers between devices  24.4 us (25%)
  waiting for transfers between devices  17.3 us (18%)
  Pallas kernels  15.7 us (16%)
    all_gather x1, blocking collectives, gather(): return lax.all_gather(both, 'z', axis=0, tiled=True)  37.5 us
    ppermute x3, starting transfers between devices, swap(): return lax.ppermute(value, axis, [(0, 1), (1, 0)])  17.3 us
    ppermute x3, waiting for transfers between devices, swap(): return lax.ppermute(value, axis, [(0, 1), (1, 0)])  17.3 us
    pallas_call x2, Pallas kernels, reduced(): pl.pallas_call(functools.partial(reduce_kernel, first_row), out_shape=jax...  7.57 us
    all_to_all x1, starting transfers between devices, shards(): lax.all_to_all(copies, CHIP, 0, 0, tiled=True).reshape(half, col_width)  7.04 us
    pallas_call x1, Pallas kernels, front(): pl.pallas_call(front_kernel, out_shape=(jax.ShapeDtypeStruct((chips, *red...  4.75 us
    pallas_call x1, Pallas kernels, ranks(): pl.pallas_call(ranks_kernel, out_shape=(grid, grid, grid, jax.ShapeDtypeS...  2.3 us
  transfers between devices with their start and end apart: 4, of which 2 were waited for; matrix products, arithmetic and copies ran while one was open for 0% of the time, Pallas kernels for 6%

profile of v6, /device:TPU:3, one launch (start us, length us, event | category | flops | bytes accessed | tf_op | source)
XLA Modules:
  0.0 95.9 jit_solution(9167008130636033153)
XLA Ops:
  0.0 4.7 %front.1 = (bf16[8,128,1024]{2,1,0:T(8,128)(2,1)}, bf16[512,1024]{1,0:T(8,128)(2,1)S(1)}, s16[96,512]{1,0:T(8,128)(2,1)}, s16[96,512]{1,0:T(8,128)(2,1)}, f32[2,1024]{1,0:T(2,128)S(1)}) custom-call(s32[16]{0:T(128)} %counts.1, s32[2,1024]{1,0:T(2,128)} %pivots.3, s32[512,1024]{1,0:T(8,128)} %rows_in.1, s32[128,1024]{1,0:T(8,128)} %bitcast.22), custom_call_target="tpu_custom_call" | custom-call | tf_op jit(solution)/shard_map/front/pallas_call | solution.py:236
  4.8 0.0 copy-start.2
  4.8 0.0 copy-start.1
  4.8 0.0 copy-start
  4.8 7.0 %all-to-all-start = ((bf16[8,128,1024]{2,1,0:T(8,128)(2,1)}), bf16[8,128,1024]{2,1,0:T(8,128)(2,1)}, u32[]{:S(2)}, u32[]{:S(2)}) async-start(bf16[8,128,1024]{2,1,0:T(8,128)(2,1)} %get-tuple-element.131), calls=%async_computation | async-start | bytes 4194304 | tf_op jit(solution)/shard_map/all_to_all | solution.py:309
  11.8 0.0 copy-done.2
  11.8 5.8 %collective-permute-start.3 = (s16[96,512]{1,0:T(8,128)(2,1)S(1)}, s16[96,512]{1,0:T(8,128)(2,1)S(1)}, u32[]{:S(2)}, u32[]{:S(2)}) collective-permute-start(s16[96,512]{1,0:T(8,128)(2,1)S(1)} %copy-done.2), channel_id=1, source_target_pairs={{0,32},{32,0},{1,33},{33,1},{2,34},{34,2},{3,35},{35,3},{4,36},{36... | collective-permute-start | bytes 294920 | tf_op jit(solution)/shard_map/ppermute | solution.py:39
  17.6 0.9 collective-permute-done.3
  18.5 0.0 copy-done.1
  18.6 1.9 %collective-permute-start.4 = (s16[96,512]{1,0:T(8,128)(2,1)S(1)}, s16[96,512]{1,0:T(8,128)(2,1)S(1)}, u32[]{:S(2)}, u32[]{:S(2)}) collective-permute-start(s16[96,512]{1,0:T(8,128)(2,1)S(1)} %add.70), channel_id=1, source_target_pairs={{0,16},{16,0},{1,17},{17,1},{2,18},{18,2},{3,19},{19,3},{4,20},{20... | collective-permute-start | bytes 294920 | tf_op jit(solution)/shard_map/ppermute | solution.py:39
  20.5 0.0 copy-done
  20.5 2.3 %ranks.1 = (s32[8,128]{1,0:T(8,128)S(1)}, s32[8,128]{1,0:T(8,128)S(1)}, s32[8,128]{1,0:T(8,128)S(1)}, s32[1]{0:T(128)}) custom-call(s32[2,1024]{1,0:T(2,128)S(1)} %copy-done), custom_call_target="tpu_custom_call" | custom-call | flops 2000000000 | bytes 1000000 | tf_op jit(solution)/shard_map/ranks/pallas_call | solution.py:260
  22.8 16.4 %collective-permute-done.4 = s16[96,512]{1,0:T(8,128)(2,1)S(1)} collective-permute-done((s16[96,512]{1,0:T(8,128)(2,1)S(1)}, s16[96,512]{1,0:T(8,128)(2,1)S(1)}, u32[]{:S(2)}, u32[]{:S(2)}) %collective-permute-start.4) | collective-permute-done | bytes 98336 | tf_op jit(solution)/shard_map/ppermute | solution.py:39
  39.2 37.5 %all-gather.2.spread = s16[1536,512]{1,0:T(8,128)(2,1)S(1)} all-gather(s16[96,512]{1,0:T(8,128)(2,1)S(1)} %add.71), channel_id=1, replica_groups=mesh['yh'=2,'x'=4,'core'=2,'yl'=2,'z'=16] {'z'}, dimensions={0}, use_global_device_ids=true | all-gather | bytes 1671168 | tf_op jit(solution)/shard_map/all_gather | solution.py:307
  76.7 0.0 all-to-all-done
  76.7 3.8 %shard_map.47 = bf16[256,1024]{1,0:T(8,128)(2,1)S(1)} custom-call(s16[1536,512]{1,0:T(8,128)(2,1)S(1)} %all-gather.2.spread, s32[8,128]{1,0:T(8,128)S(1)} %get-tuple-element.129.where, bf16[512,1024]{1,0:T(8,128)(2,1)S(1)} %get-tuple-element.210.placed, bf16[1024,1024]{1,0:T(8,128)(2,1)} %bitcast.5.panel_in), custom_call_target="tpu_custom_call" | custom-call | flops 1500000000 | bytes 5000000 | tf_op jit(solution)/shard_map/pallas_call | solution.py:273
  80.5 9.6 %collective-permute-start.5 = (bf16[256,1024]{1,0:T(8,128)(2,1)S(1)}, bf16[256,1024]{1,0:T(8,128)(2,1)S(1)}, u32[]{:S(2)}, u32[]{:S(2)}) collective-permute-start(bf16[256,1024]{1,0:T(8,128)(2,1)S(1)} %shard_map.47), channel_id=1, source_target_pairs={{0,32},{32,0},{1,33},{33,1},{2,34},{34,2},{3,35},{35,3},{4,36},{36... | collective-permute-start | bytes 1572872 | tf_op jit(solution)/shard_map/ppermute | solution.py:39
  90.1 3.8 %shard_map.46.own = bf16[256,1024]{1,0:T(8,128)(2,1)S(1)} custom-call(s16[1536,512]{1,0:T(8,128)(2,1)S(1)} %all-gather.2.spread, s32[8,128]{1,0:T(8,128)S(1)} %get-tuple-element.129.where, bf16[512,1024]{1,0:T(8,128)(2,1)S(1)} %get-tuple-element.210.placed, bf16[1024,1024]{1,0:T(8,128)(2,1)} %bitcast.5.panel_in), custom_call_target="tpu_custom_call" | custom-call | flops 1500000000 | bytes 5000000 | tf_op jit(solution)/shard_map/pallas_call | solution.py:273
  93.9 0.0 collective-permute-done.5.incoming
  93.9 1.1 %combine.1 = s32[256,1024]{1,0:T(8,128)} custom-call(bf16[256,1024]{1,0:T(8,128)(2,1)S(1)} %shard_map.46.own, bf16[256,1024]{1,0:T(8,128)(2,1)S(1)} %collective-permute-done.5.incoming), custom_call_target="tpu_custom_call" | custom-call | tf_op jit(solution)/shard_map/combine/pallas_call | solution.py:285
  95.0 0.8 while.13
  (2 shorter events, 0.1 us)
Async XLA Ops:
  4.8 7.1 %copy-start.2 = (s16[96,512]{1,0:T(8,128)(2,1)S(1)}, s16[96,512]{1,0:T(8,128)(2,1)}, u32[]{:S(2)}) copy-start(s16[96,512]{1,0:T(8,128)(2,1)} %get-tuple-element.128) | copy-start | bytes 294916
  4.8 13.8 %copy-start.1 = (s16[96,512]{1,0:T(8,128)(2,1)S(1)}, s16[96,512]{1,0:T(8,128)(2,1)}, u32[]{:S(2)}) copy-start(s16[96,512]{1,0:T(8,128)(2,1)} %get-tuple-element.127) | copy-start | bytes 294916
  4.8 15.7 %copy-start = (s32[2,1024]{1,0:T(2,128)S(1)}, s32[2,1024]{1,0:T(2,128)}, u32[]{:S(2)}) copy-start(s32[2,1024]{1,0:T(2,128)} %pivots.3) | copy-start | bytes 24580
  4.8 71.9 %all-to-all-start = ((bf16[8,128,1024]{2,1,0:T(8,128)(2,1)}), bf16[8,128,1024]{2,1,0:T(8,128)(2,1)}, u32[]{:S(2)}, u32[]{:S(2)}) async-start(bf16[8,128,1024]{2,1,0:T(8,128)(2,1)} %get-tuple-element.131), calls=%async_computation | async-start | bytes 4194304 | tf_op jit(solution)/shard_map/all_to_all | solution.py:309
  11.8 6.7 %collective-permute-start.3 = (s16[96,512]{1,0:T(8,128)(2,1)S(1)}, s16[96,512]{1,0:T(8,128)(2,1)S(1)}, u32[]{:S(2)}, u32[]{:S(2)}) collective-permute-start(s16[96,512]{1,0:T(8,128)(2,1)S(1)} %copy-done.2), channel_id=1, source_target_pairs={{0,32},{32,0},{1,33},{33,1},{2,34},{34,2},{3,35},{35,3},{4,36},{36... | collective-permute-start | bytes 294920 | tf_op jit(solution)/shard_map/ppermute | solution.py:39
  18.6 20.6 %collective-permute-start.4 = (s16[96,512]{1,0:T(8,128)(2,1)S(1)}, s16[96,512]{1,0:T(8,128)(2,1)S(1)}, u32[]{:S(2)}, u32[]{:S(2)}) collective-permute-start(s16[96,512]{1,0:T(8,128)(2,1)S(1)} %add.70), channel_id=1, source_target_pairs={{0,16},{16,0},{1,17},{17,1},{2,18},{18,2},{3,19},{19,3},{4,20},{20... | collective-permute-start | bytes 294920 | tf_op jit(solution)/shard_map/ppermute | solution.py:39
  80.5 13.4 %collective-permute-start.5 = (bf16[256,1024]{1,0:T(8,128)(2,1)S(1)}, bf16[256,1024]{1,0:T(8,128)(2,1)S(1)}, u32[]{:S(2)}, u32[]{:S(2)}) collective-permute-start(bf16[256,1024]{1,0:T(8,128)(2,1)S(1)} %shard_map.47), channel_id=1, source_target_pairs={{0,32},{32,0},{1,33},{33,1},{2,34},{34,2},{3,35},{35,3},{4,36},{36... | collective-permute-start | bytes 1572872 | tf_op jit(solution)/shard_map/ppermute | solution.py:39

commit v7 on v6

--- a/solution.py
+++ b/solution.py
@@ -57,15 +57,7 @@
     return one_hot(lower < upper)
 
 
-def front_kernel(
-    counts, pivots, rows_in, reducers_in, copies, placed, keep, send, slots, rows, reducers, normed, done, come
-):
-    reads = [
-        pltpu.make_async_copy(reducers_in, reducers, come.at[0]),
-        pltpu.make_async_copy(rows_in, rows, come.at[1]),
-    ]
-    for read in reads:
-        read.start()
+def front_kernel(counts, pivots, rows, reducers, copies, placed, keep, send, slots, normed, done):
     width = rows.shape[1]
     capacity = rows.shape[0]
     groups = width // LANES
@@ -111,7 +103,6 @@
     target = (row_ids & (part - 1)) + part * core
     own_pivot = jnp.sum(jnp.where(lane_ids == target, chosen, 0.0), axis=1, keepdims=True)
     base = start.astype(jnp.float32)
-    reads[0].wait()
     for group in range(groups):
         cols = slice(group * LANES, (group + 1) * LANES)
         here = (lane_ids + group * LANES).astype(jnp.float32) + base
@@ -128,7 +119,6 @@
     places = lax.broadcasted_iota(jnp.int32, (capacity, capacity), 0)
     places = (places + LIVE_DEV * core) & (capacity - 1)
     pick = one_hot((slot_ids < mine) & (slot_ids == places - core * first))
-    reads[1].wait()
     values = rows[...].astype(jnp.float32).astype(jnp.bfloat16)
     values = dot(pick, values, NN).astype(jnp.bfloat16)
     placed[...] = values
@@ -137,8 +127,10 @@
     here = jnp.where(core == 0, columns[0], columns[1])
     there = jnp.where(core == 0, columns[1], columns[0])
     slots[0:1, :], slots[1:2, :] = here, there
-    keep[...] = centered(dot(one_hot(here == want), values, NT)).astype(jnp.int32).astype(jnp.int16)
-    other = centered(dot(one_hot(there == want), values, NT)).astype(jnp.int32).astype(jnp.int16)
+    choose = jnp.concatenate([one_hot(here == want), one_hot(there == want)], axis=0)
+    packed = centered(dot(choose, values, NT)).astype(jnp.int32).astype(jnp.int16)
+    keep[...] = packed[:CAP]
+    other = packed[CAP:]
     send[:, :LIVE_DEV] = other[:, LIVE_DEV:]
     send[:, LIVE_DEV:] = other[:, :LIVE_DEV]
     for write in writes:
@@ -149,66 +141,74 @@
     core = lax.axis_index("core")
     count = pivots.shape[1]
     chunks = 32768 // LANES
-    both = 2 * LANES
-    lane_rows = lax.broadcasted_iota(jnp.int32, (both, count), 0)
-    chunk_rows = lax.broadcasted_iota(jnp.int32, (chunks, count), 0)
+    pieces = count // LANES
+
+    pair_rows = lax.broadcasted_iota(jnp.int32, (32, count), 0)
     side = (lax.broadcasted_iota(jnp.int32, (1, count), 1) >> 6) & 1
-    chunk_marks = []
-    marks = jnp.zeros((chunks, both), jnp.float32)
+    counted = jnp.zeros((32, 1), jnp.float32)
+    grids = []
     for panel in range(PANELS):
         pivot = pivots[panel:panel + 1, :]
-        chunk_marks.append(one_hot(chunk_rows == (pivot >> 7)))
-        marks += dot(chunk_marks[-1], one_hot(lane_rows == ((pivot & (LANES - 1)) + side * LANES)), NT)
-    flags = marks.astype(jnp.bfloat16)
+        hits = (pair_rows == ((pivot >> 10) & 15) + 16 * side).astype(jnp.float32)
+        counted += jnp.sum(hits, axis=1, keepdims=True)
+        grids.append(jnp.concatenate([pivot[:, i * LANES:(i + 1) * LANES] for i in range(pieces)], axis=0))
+    extra[0] = (jnp.max(counted).astype(jnp.int32) - 1) // CAP
+
+    left = lax.broadcasted_iota(jnp.int32, grids[0].shape, 1) < LANES // 2
+    lows = jnp.where(left, grids[0], pltpu.roll(grids[1], LANES // 2, axis=1))
+    highs = jnp.where(left, pltpu.roll(grids[0], LANES // 2, axis=1), grids[1])
+    own = jnp.where(core == 0, lows, highs)
+    pivot = spread_row(own)
+    chunk_hot = one_hot(lax.broadcasted_iota(jnp.int32, (chunks, count), 0) == (pivot >> 7))
+    lane_hits = lax.broadcasted_iota(jnp.int32, (LANES, count), 0) == (pivot & (LANES - 1))
+    flags = dot(chunk_hot, one_hot(lane_hits), NT).astype(jnp.bfloat16)
     here = lax.broadcasted_iota(jnp.int32, (chunks, chunks), 0)
     other = lax.broadcasted_iota(jnp.int32, (chunks, chunks), 1)
     block, other_block = here >> 3, other >> 3
     earlier = one_hot(((block == other_block) & (other < here)) | (block == other_block + 16))
-    same_side = (here >> 7) == (other >> 7)
-    totals = dot(flags, one_hot(same_side), NN).astype(jnp.bfloat16)
-    table = dot(flags, one_hot(same_side & (here < other)), NN) + dot(earlier, totals, NN)
-    extra[0] = jnp.max(jnp.where(marks > 0.0, table, 0.0)).astype(jnp.int32) // CAP
-    table = jnp.where(core == 0, table[:, :LANES], table[:, LANES:])
+    totals = dot(flags, jnp.ones((LANES, LANES), jnp.bfloat16), NN).astype(jnp.bfloat16)
+    table = dot(flags, strictly_before(LANES), NN) + dot(earlier, totals, NN)
     high = jnp.floor(table * (1.0 / 128.0))
     parts = jnp.concatenate([high, table - 128.0 * high], axis=1).astype(jnp.bfloat16)
-    grids = []
-    for panel in range(PANELS):
-        pivot = pivots[panel:panel + 1, :]
-        found = dot(parts, chunk_marks[panel], TN)
-        found = 128.0 * found[:LANES] + found[LANES:]
-        rank = jnp.where(lane_rows[:LANES] == (pivot & (LANES - 1)), found, 0.0)
-        rank = jnp.sum(rank, axis=0, keepdims=True).astype(jnp.int32)
-        for value in (rank, ((pivot >> 10) & 15) * CAP + rank):
-            grids.append(jnp.concatenate([value[:, i * LANES:(i + 1) * LANES] for i in range(count // LANES)], axis=0))
-    left = lax.broadcasted_iota(jnp.int32, grids[0].shape, 1) < LANES // 2
-    picked = []
-    for a, b in ((grids[0], grids[2]), (grids[1], grids[3])):
-        lows = jnp.where(left, a, pltpu.roll(b, LANES // 2, axis=1))
-        highs = jnp.where(left, pltpu.roll(a, LANES // 2, axis=1), b)
-        picked.append(jnp.where(core == 0, lows, highs))
-    ranks[...], slots[...] = picked
-    firsts[...] = jnp.where(picked[0] < CAP, picked[1], -1)
-
-
-def reduce_kernel(first_row, spread, where, placed, panel_in, out, panel, come):
-    depth = 2 * LANES
-    blocks = panel.shape[0] // depth
-    reads = []
-    for block in range(blocks):
-        part = pl.ds(block * depth, depth)
-        reads.append(pltpu.make_async_copy(panel_in.at[part], panel.at[part], come.at[block]))
-        reads[block].start()
-    rows = slice(first_row, first_row + LIVE_DEV)
+    found = dot(parts, chunk_hot, TN)
+    found = 128.0 * found[:LANES] + found[LANES:]
+    rank = jnp.sum(jnp.where(lane_hits, found, 0.0), axis=0, keepdims=True).astype(jnp.int32)
+    rank = jnp.concatenate([rank[:, i * LANES:(i + 1) * LANES] for i in range(pieces)], axis=0)
+    slot = ((own >> 10) & 15) * CAP + rank
+    ranks[...] = rank
+    slots[...] = slot
+    firsts[...] = jnp.where(rank < CAP, slot, -1)
+
+
+def unpack_kernel(spread, where, factors):
     slot_count = spread.shape[0]
-    packed = jnp.transpose(spread[:, rows].astype(jnp.int32).astype(jnp.float32)).astype(jnp.bfloat16)
-    slot_rows = lax.broadcasted_iota(jnp.int32, (slot_count, depth), 0)
-    total = jnp.zeros(out.shape, jnp.float32)
-    for block in range(blocks):
-        here = spread_row(where[2 * block:2 * block + 2, :])
-        factors = dot(packed, one_hot(slot_rows == here), NN).astype(jnp.bfloat16)
-        reads[block].wait()
-        total += dot(factors, panel[block * depth:(block + 1) * depth, :], NN)
-    out[...] = remainder(placed[rows, :].astype(jnp.float32) - total).astype(jnp.bfloat16)
+    packed = spread[...].astype(jnp.int32).astype(jnp.float32).astype(jnp.bfloat16)
+    slot_lanes = lax.broadcasted_iota(jnp.int32, (2 * LANES, slot_count), 1)
+    square = (LANES, LANES)
+    diagonal = lax.broadcasted_iota(jnp.int32, square, 0) == lax.broadcasted_iota(jnp.int32, square, 1)
+    for block in range(where.shape[0] // 2):
+        columns = [
+            jnp.sum(
+                jnp.where(diagonal, where[piece:piece + 1, :].astype(jnp.float32), 0.0), axis=1, keepdims=True
+            )
+            for piece in (2 * block, 2 * block + 1)
+        ]
+        here = jnp.concatenate(columns, axis=0).astype(jnp.int32)
+        rows = slice(block * 2 * LANES, (block + 1) * 2 * LANES)
+        factors[rows, :] = dot(one_hot(slot_lanes == here), packed, NN).astype(jnp.bfloat16)
+
+
+def reduce_kernel(first_row, factors, placed, panel, out, values, come):
+    read = pltpu.make_async_copy(placed.at[pl.ds(first_row, LIVE_DEV)], values, come)
+    read.start()
+    turned = jnp.transpose(factors[:, first_row:first_row + LIVE_DEV])
+    step = panel.shape[1] // 4
+    for part in range(4):
+        cols = slice(part * step, (part + 1) * step)
+        product = dot(turned, panel[:, cols], NN)
+        if part == 0:
+            read.wait()
+        out[:, cols] = remainder(values[:, cols].astype(jnp.float32) - product).astype(jnp.bfloat16)
 
 
 def combine_kernel(own, incoming, out, result, done):
@@ -242,14 +242,11 @@
             packed,
             jax.ShapeDtypeStruct((2, width), jnp.float32),
         ),
-        in_specs=[SMEM, VMEM, ANY, ANY],
+        in_specs=[SMEM, VMEM, VMEM, VMEM],
         out_specs=(ANY, VMEM, VMEM, VMEM, VMEM),
         scratch_shapes=[
-            pltpu.VMEM(rows.shape, jnp.int32),
-            pltpu.VMEM(reducers.shape, jnp.int32),
             pltpu.VMEM(reducers.shape, jnp.bfloat16),
             pltpu.SemaphoreType.DMA((chips,)),
-            pltpu.SemaphoreType.DMA((2,)),
         ],
         name="front",
     )(counts, pivots, rows, reducers)
@@ -268,17 +265,29 @@
     )(pivots)
 
 
-def reduced(first_row, spread, where, placed, panel):
+def unpacked(spread, where):
+    return pl.pallas_call(
+        unpack_kernel,
+        out_shape=jax.ShapeDtypeStruct((where.shape[0] * LANES, spread.shape[1]), jnp.bfloat16),
+        in_specs=[VMEM] * 2,
+        out_specs=VMEM,
+        name="unpack",
+        compiler_params=pltpu.CompilerParams(vmem_limit_bytes=24 << 20),
+        cost_estimate=pl.CostEstimate(flops=1_600_000_000, bytes_accessed=3_000_000, transcendentals=0),
+    )(spread, where)
+
+
+def reduced(first_row, factors, placed, panel):
     width = panel.shape[1]
     return pl.pallas_call(
         functools.partial(reduce_kernel, first_row),
         out_shape=jax.ShapeDtypeStruct((LIVE_DEV, width), jnp.bfloat16),
-        in_specs=[VMEM, VMEM, VMEM, ANY],
+        in_specs=[VMEM, ANY, VMEM],
         out_specs=VMEM,
-        scratch_shapes=[pltpu.VMEM(panel.shape, jnp.bfloat16), pltpu.SemaphoreType.DMA((panel.shape[0] // (2 * LANES),))],
+        scratch_shapes=[pltpu.VMEM((LIVE_DEV, width), jnp.bfloat16), pltpu.SemaphoreType.DMA],
         compiler_params=pltpu.CompilerParams(vmem_limit_bytes=24 << 20),
-        cost_estimate=pl.CostEstimate(flops=1_500_000_000, bytes_accessed=5_000_000, transcendentals=0),
-    )(spread, where, placed, panel)
+        cost_estimate=pl.CostEstimate(flops=540_000_000, bytes_accessed=4_000_000, transcendentals=0),
+    )(factors, placed, panel)
 
 
 def combine(own, incoming):
@@ -298,7 +307,8 @@
     col_width = pair_rows.shape[1]
     rows_dev = PANELS * reducers.shape[1]
     half = chips * rows_dev
-    copies, placed, keep, send, columns = front(counts, pivots, pair_rows, reducers.reshape(rows_dev, col_width), chips)
+    blocks = (counts, pivots, pair_rows, reducers.reshape(rows_dev, col_width))
+    copies, placed, keep, send, columns = front(*blocks, chips)
     my_rank, my_slot, firsts, extra = ranks(pivots)
 
     def gather(keep, send):
@@ -306,11 +316,19 @@
         both = both + swap(both, "yl")
         return lax.all_gather(both, "z", axis=0, tiled=True)
 
-    panel = lax.all_to_all(copies, CHIP, 0, 0, tiled=True).reshape(half, col_width)
+    def fetch_panel(copies):
+        return lax.all_to_all(copies, CHIP, 0, 0, tiled=True).reshape(half, col_width)
+
+    def unpack(spread, where):
+        table = (where.reshape(-1, 1) == lax.iota(jnp.int32, spread.shape[0])[None, :]).astype(jnp.bfloat16)
+        return dot(table, spread.astype(jnp.bfloat16), NN).astype(jnp.bfloat16)
+
+    panel = fetch_panel(copies)
     spread = gather(keep, send)
-    incoming = reduced(LIVE_DEV, spread, firsts, placed, panel)
-    incoming = swap(incoming, "core")
-    own = reduced(0, spread, firsts, placed, panel)
+
+    factors = unpacked(spread, firsts)
+    incoming = swap(reduced(LIVE_DEV, factors, placed, panel), "core")
+    own = reduced(0, factors, placed, panel)
     first = combine(own, incoming)
 
     def another(state):
@@ -321,10 +339,10 @@
             centered(dot((columns[side] == want[:, None]).astype(jnp.bfloat16), placed, NT)).astype(jnp.int16)
             for side in range(2)
         ]
-        spread = gather(keep, jnp.roll(send, LIVE_DEV, axis=1)).astype(jnp.bfloat16)
-        where = jnp.where((my_rank >= base) & (my_rank < base + CAP), my_slot - base, -1).reshape(-1, 1)
-        table = (where == lax.iota(jnp.int32, spread.shape[0])[None, :]).astype(jnp.bfloat16)
-        products = remainder(dot(dot(table, spread, NN).astype(jnp.bfloat16), panel, TN))
+        where = jnp.where((my_rank >= base) & (my_rank < base + CAP), my_slot - base, -1)
+        factors = unpack(gather(keep, jnp.roll(send, LIVE_DEV, axis=1)), where)
+        again, _ = lax.optimization_barrier((copies, step))
+        products = remainder(dot(factors, fetch_panel(again), TN))
         incoming = swap(products[LIVE_DEV:].astype(jnp.bfloat16), "core").astype(jnp.float32)
         result = result.astype(jnp.float32) - products[:LIVE_DEV] - incoming
         return step - 1, remainder(result).astype(jnp.int32)

time: 96.3 us -> 94.9 us (0.985)
  the two profiles are of different devices: /device:TPU:3 before, /device:TPU:19 now
where the time goes in v7:
time: 94.9 us; the launch traced here: 94.5 us
  blocking collectives  37.5 us (40%)
  starting transfers between devices  23.1 us (24%)
  waiting for transfers between devices  19.1 us (20%)
  Pallas kernels  13.2 us (14%)
    all_gather x1, blocking collectives, gather(): return lax.all_gather(both, 'z', axis=0, tiled=True)  37.5 us
    ppermute x3, waiting for transfers between devices, swap(): return lax.ppermute(value, axis, [(0, 1), (1, 0)])  19.1 us
    ppermute x3, starting transfers between devices, swap(): return lax.ppermute(value, axis, [(0, 1), (1, 0)])  16.3 us
    all_to_all x1, starting transfers between devices, fetch_panel(): lax.all_to_all(copies, CHIP, 0, 0, tiled=True).reshape(half, col_width)  6.82 us
    pallas_call x1, Pallas kernels, front(): pl.pallas_call(front_kernel, out_shape=(jax.ShapeDtypeStruct((chips, *red...  4.62 us
    pallas_call x2, Pallas kernels, reduced(): pl.pallas_call(functools.partial(reduce_kernel, first_row), out_shape=jax...  3.71 us
    pallas_call x1, Pallas kernels, unpacked(): pl.pallas_call(unpack_kernel, out_shape=jax.ShapeDtypeStruct((where.shape...  2.04 us
  transfers between devices with their start and end apart: 4, of which 2 were waited for; matrix products, arithmetic and copies ran while one was open for 0% of the time, Pallas kernels for 6%

profile of v7, /device:TPU:19, one launch (start us, length us, event | category | flops | bytes accessed | tf_op | source)
XLA Modules:
  0.0 94.5 jit_solution(11990508274917522247)
XLA Ops:
  0.0 4.6 %front.1 = (bf16[8,128,1024]{2,1,0:T(8,128)(2,1)}, bf16[512,1024]{1,0:T(8,128)(2,1)}, s16[96,512]{1,0:T(8,128)(2,1)}, s16[96,512]{1,0:T(8,128)(2,1)}, f32[2,1024]{1,0:T(2,128)S(1)}) custom-call(s32[16]{0:T(128)} %counts.1, s32[2,1024]{1,0:T(2,128)} %pivots.3, s32[512,1024]{1,0:T(8,128)} %rows.1, s32[128,1024]{1,0:T(8,128)} %bitcast.28), custom_call_target="tpu_custom_call" | custom-call | tf_op jit(solution)/shard_map/front/pallas_call | solution.py:236
  4.6 0.0 copy-start.4
  4.6 0.0 copy-start.3
  4.7 0.0 copy-start
  4.7 6.8 %all-to-all-start.1 = ((bf16[8,128,1024]{2,1,0:T(8,128)(2,1)}), bf16[8,128,1024]{2,1,0:T(8,128)(2,1)S(1)}, u32[]{:S(2)}, u32[]{:S(2)}) async-start(bf16[8,128,1024]{2,1,0:T(8,128)(2,1)} %get-tuple-element.214), calls=%async_computation.1 | async-start | bytes 4194304 | tf_op jit(solution)/shard_map/all_to_all | solution.py:320
  11.5 0.0 copy-done.4
  11.5 5.1 %collective-permute-start.3 = (s16[96,512]{1,0:T(8,128)(2,1)S(1)}, s16[96,512]{1,0:T(8,128)(2,1)S(1)}, u32[]{:S(2)}, u32[]{:S(2)}) collective-permute-start(s16[96,512]{1,0:T(8,128)(2,1)S(1)} %copy-done.4), channel_id=1, source_target_pairs={{0,32},{32,0},{1,33},{33,1},{2,34},{34,2},{3,35},{35,3},{4,36},{36... | collective-permute-start | bytes 294920 | tf_op jit(solution)/shard_map/ppermute | solution.py:39
  16.6 0.9 collective-permute-done.3
  17.5 0.0 copy-done.3
  17.5 1.9 %collective-permute-start.4 = (s16[96,512]{1,0:T(8,128)(2,1)S(1)}, s16[96,512]{1,0:T(8,128)(2,1)S(1)}, u32[]{:S(2)}, u32[]{:S(2)}) collective-permute-start(s16[96,512]{1,0:T(8,128)(2,1)S(1)} %add.70), channel_id=1, source_target_pairs={{0,16},{16,0},{1,17},{17,1},{2,18},{18,2},{3,19},{19,3},{4,20},{20... | collective-permute-start | bytes 294920 | tf_op jit(solution)/shard_map/ppermute | solution.py:39
  19.5 0.0 copy-done
  19.5 1.8 %ranks.1 = (s32[8,128]{1,0:T(8,128)S(1)}, s32[8,128]{1,0:T(8,128)S(1)}, s32[8,128]{1,0:T(8,128)S(1)}, s32[1]{0:T(128)}) custom-call(s32[2,1024]{1,0:T(2,128)S(1)} %copy-done), custom_call_target="tpu_custom_call" | custom-call | flops 2000000000 | bytes 1000000 | tf_op jit(solution)/shard_map/ranks/pallas_call | solution.py:257
  21.2 18.1 %collective-permute-done.4 = s16[96,512]{1,0:T(8,128)(2,1)S(1)} collective-permute-done((s16[96,512]{1,0:T(8,128)(2,1)S(1)}, s16[96,512]{1,0:T(8,128)(2,1)S(1)}, u32[]{:S(2)}, u32[]{:S(2)}) %collective-permute-start.4) | collective-permute-done | bytes 98336 | tf_op jit(solution)/shard_map/ppermute | solution.py:39
  39.4 37.5 %all-gather.2.spread = s16[1536,512]{1,0:T(8,128)(2,1)S(1)} all-gather(s16[96,512]{1,0:T(8,128)(2,1)S(1)} %add.71), channel_id=1, replica_groups=mesh['yh'=2,'x'=4,'core'=2,'yl'=2,'z'=16] {'z'}, dimensions={0}, use_global_device_ids=true | all-gather | bytes 1671168 | tf_op jit(solution)/shard_map/all_gather | solution.py:317
  76.8 2.0 %unpack.1.factors = bf16[1024,512]{1,0:T(8,128)(2,1)S(1)} custom-call(s16[1536,512]{1,0:T(8,128)(2,1)S(1)} %all-gather.2.spread, s32[8,128]{1,0:T(8,128)S(1)} %get-tuple-element.130.where), custom_call_target="tpu_custom_call" | custom-call | flops 1600000000 | bytes 3000000 | tf_op jit(solution)/shard_map/unpack/pallas_call | solution.py:269
  78.9 0.0 all-to-all-done.1
  78.9 0.0 copy-start.1
  78.9 2.3 %shard_map.47 = bf16[256,1024]{1,0:T(8,128)(2,1)S(1)} custom-call(bf16[1024,512]{1,0:T(8,128)(2,1)S(1)} %unpack.1.factors, bf16[512,1024]{1,0:T(8,128)(2,1)} %get-tuple-element.213.placed, bf16[1024,1024]{1,0:T(8,128)(2,1)S(1)} %bitcast.25), custom_call_target="tpu_custom_call" | custom-call | flops 540000000 | bytes 4000000 | tf_op jit(solution)/shard_map/pallas_call | solution.py:282
  81.2 9.3 %collective-permute-start.5 = (bf16[256,1024]{1,0:T(8,128)(2,1)S(1)}, bf16[256,1024]{1,0:T(8,128)(2,1)S(1)}, u32[]{:S(2)}, u32[]{:S(2)}) collective-permute-start(bf16[256,1024]{1,0:T(8,128)(2,1)S(1)} %shard_map.47), channel_id=1, source_target_pairs={{0,32},{32,0},{1,33},{33,1},{2,34},{34,2},{3,35},{35,3},{4,36},{36... | collective-permute-start | bytes 1572872 | tf_op jit(solution)/shard_map/ppermute | solution.py:39
  90.5 1.4 %shard_map.46.own = bf16[256,1024]{1,0:T(8,128)(2,1)S(1)} custom-call(bf16[1024,512]{1,0:T(8,128)(2,1)S(1)} %unpack.1.factors, bf16[512,1024]{1,0:T(8,128)(2,1)S(1)} %copy-done.1, bf16[1024,1024]{1,0:T(8,128)(2,1)S(1)} %bitcast.26), custom_call_target="tpu_custom_call" | custom-call | flops 540000000 | bytes 4000000 | tf_op jit(solution)/shard_map/pallas_call | solution.py:282
  92.0 0.0 collective-permute-done.5.incoming
  92.0 1.1 %combine.1 = s32[256,1024]{1,0:T(8,128)} custom-call(bf16[256,1024]{1,0:T(8,128)(2,1)S(1)} %shard_map.46.own, bf16[256,1024]{1,0:T(8,128)(2,1)S(1)} %collective-permute-done.5.incoming), custom_call_target="tpu_custom_call" | custom-call | tf_op jit(solution)/shard_map/combine/pallas_call | solution.py:294
  93.1 0.5 copy-done.2
  93.6 0.8 while.13
  (4 shorter events, 0.1 us)
Async XLA Ops:
  4.6 6.9 %copy-start.4 = (s16[96,512]{1,0:T(8,128)(2,1)S(1)}, s16[96,512]{1,0:T(8,128)(2,1)}, u32[]{:S(2)}) copy-start(s16[96,512]{1,0:T(8,128)(2,1)} %get-tuple-element.129) | copy-start | bytes 294916
  4.6 12.9 %copy-start.3 = (s16[96,512]{1,0:T(8,128)(2,1)S(1)}, s16[96,512]{1,0:T(8,128)(2,1)}, u32[]{:S(2)}) copy-start(s16[96,512]{1,0:T(8,128)(2,1)} %get-tuple-element.128) | copy-start | bytes 294916
  4.7 14.8 %copy-start = (s32[2,1024]{1,0:T(2,128)S(1)}, s32[2,1024]{1,0:T(2,128)}, u32[]{:S(2)}) copy-start(s32[2,1024]{1,0:T(2,128)} %pivots.3) | copy-start | bytes 24580
  4.7 74.2 %all-to-all-start.1 = ((bf16[8,128,1024]{2,1,0:T(8,128)(2,1)}), bf16[8,128,1024]{2,1,0:T(8,128)(2,1)S(1)}, u32[]{:S(2)}, u32[]{:S(2)}) async-start(bf16[8,128,1024]{2,1,0:T(8,128)(2,1)} %get-tuple-element.214), calls=%async_computation.1 | async-start | bytes 4194304 | tf_op jit(solution)/shard_map/all_to_all | solution.py:320
  11.5 6.0 %collective-permute-start.3 = (s16[96,512]{1,0:T(8,128)(2,1)S(1)}, s16[96,512]{1,0:T(8,128)(2,1)S(1)}, u32[]{:S(2)}, u32[]{:S(2)}) collective-permute-start(s16[96,512]{1,0:T(8,128)(2,1)S(1)} %copy-done.4), channel_id=1, source_target_pairs={{0,32},{32,0},{1,33},{33,1},{2,34},{34,2},{3,35},{35,3},{4,36},{36... | collective-permute-start | bytes 294920 | tf_op jit(solution)/shard_map/ppermute | solution.py:39
  17.5 21.8 %collective-permute-start.4 = (s16[96,512]{1,0:T(8,128)(2,1)S(1)}, s16[96,512]{1,0:T(8,128)(2,1)S(1)}, u32[]{:S(2)}, u32[]{:S(2)}) collective-permute-start(s16[96,512]{1,0:T(8,128)(2,1)S(1)} %add.70), channel_id=1, source_target_pairs={{0,16},{16,0},{1,17},{17,1},{2,18},{18,2},{3,19},{19,3},{4,20},{20... | collective-permute-start | bytes 294920 | tf_op jit(solution)/shard_map/ppermute | solution.py:39
  78.9 11.6 %copy-start.1 = (bf16[512,1024]{1,0:T(8,128)(2,1)S(1)}, bf16[512,1024]{1,0:T(8,128)(2,1)}, u32[]{:S(2)}) copy-start(bf16[512,1024]{1,0:T(8,128)(2,1)} %get-tuple-element.213.placed) | copy-start | bytes 3145732
  81.2 10.8 %collective-permute-start.5 = (bf16[256,1024]{1,0:T(8,128)(2,1)S(1)}, bf16[256,1024]{1,0:T(8,128)(2,1)S(1)}, u32[]{:S(2)}, u32[]{:S(2)}) collective-permute-start(bf16[256,1024]{1,0:T(8,128)(2,1)S(1)} %shard_map.47), channel_id=1, source_target_pairs={{0,32},{32,0},{1,33},{33,1},{2,34},{34,2},{3,35},{35,3},{4,36},{36... | collective-permute-start | bytes 1572872 | tf_op jit(solution)/shard_map/ppermute | solution.py:39
  92.0 1.6 %copy-start.2 = (bf16[512,1024]{1,0:T(8,128)(2,1)S(1)}, bf16[512,1024]{1,0:T(8,128)(2,1)}, u32[]{:S(2)}) copy-start(bf16[512,1024]{1,0:T(8,128)(2,1)} %get-tuple-element.213.placed) | copy-start | bytes 3145732

commit v8 on v7

--- a/solution.py
+++ b/solution.py
@@ -180,13 +180,22 @@
     firsts[...] = jnp.where(rank < CAP, slot, -1)
 
 
-def unpack_kernel(spread, where, factors):
+def reduce_kernel(first_row, spread, where, placed, panel_in, out, values, panel, come):
+    quarter = panel.shape[0] // 4
+    reads = [pltpu.make_async_copy(placed.at[pl.ds(first_row, LIVE_DEV)], values, come.at[0])]
+    for part in range(4):
+        rows = pl.ds(part * quarter, quarter)
+        reads.append(pltpu.make_async_copy(panel_in.at[rows], panel.at[rows], come.at[part + 1]))
+    for read in reads:
+        read.start()
     slot_count = spread.shape[0]
-    packed = spread[...].astype(jnp.int32).astype(jnp.float32).astype(jnp.bfloat16)
-    slot_lanes = lax.broadcasted_iota(jnp.int32, (2 * LANES, slot_count), 1)
+    depth = 2 * LANES
+    packed = spread[:, first_row:first_row + LIVE_DEV].astype(jnp.int32).astype(jnp.float32).astype(jnp.bfloat16)
+    slot_lanes = lax.broadcasted_iota(jnp.int32, (depth, slot_count), 1)
     square = (LANES, LANES)
     diagonal = lax.broadcasted_iota(jnp.int32, square, 0) == lax.broadcasted_iota(jnp.int32, square, 1)
-    for block in range(where.shape[0] // 2):
+    turned = []
+    for block in range(panel.shape[0] // depth):
         columns = [
             jnp.sum(
                 jnp.where(diagonal, where[piece:piece + 1, :].astype(jnp.float32), 0.0), axis=1, keepdims=True
@@ -194,20 +203,14 @@
             for piece in (2 * block, 2 * block + 1)
         ]
         here = jnp.concatenate(columns, axis=0).astype(jnp.int32)
-        rows = slice(block * 2 * LANES, (block + 1) * 2 * LANES)
-        factors[rows, :] = dot(one_hot(slot_lanes == here), packed, NN).astype(jnp.bfloat16)
-
-
-def reduce_kernel(first_row, factors, placed, panel, out, values, come):
-    read = pltpu.make_async_copy(placed.at[pl.ds(first_row, LIVE_DEV)], values, come)
-    read.start()
-    turned = jnp.transpose(factors[:, first_row:first_row + LIVE_DEV])
+        turned.append(jnp.transpose(dot(one_hot(slot_lanes == here), packed, NN).astype(jnp.bfloat16)))
+    factors = jnp.concatenate(turned, axis=1)
     step = panel.shape[1] // 4
+    for read in reads:
+        read.wait()
     for part in range(4):
         cols = slice(part * step, (part + 1) * step)
-        product = dot(turned, panel[:, cols], NN)
-        if part == 0:
-            read.wait()
+        product = dot(factors, panel[:, cols], NN)
         out[:, cols] = remainder(values[:, cols].astype(jnp.float32) - product).astype(jnp.bfloat16)
 
 
@@ -265,29 +268,21 @@
     )(pivots)
 
 
-def unpacked(spread, where):
-    return pl.pallas_call(
-        unpack_kernel,
-        out_shape=jax.ShapeDtypeStruct((where.shape[0] * LANES, spread.shape[1]), jnp.bfloat16),
-        in_specs=[VMEM] * 2,
-        out_specs=VMEM,
-        name="unpack",
-        compiler_params=pltpu.CompilerParams(vmem_limit_bytes=24 << 20),
-        cost_estimate=pl.CostEstimate(flops=1_600_000_000, bytes_accessed=3_000_000, transcendentals=0),
-    )(spread, where)
-
-
-def reduced(first_row, factors, placed, panel):
+def reduced(first_row, spread, where, placed, panel):
     width = panel.shape[1]
     return pl.pallas_call(
         functools.partial(reduce_kernel, first_row),
         out_shape=jax.ShapeDtypeStruct((LIVE_DEV, width), jnp.bfloat16),
-        in_specs=[VMEM, ANY, VMEM],
+        in_specs=[VMEM, VMEM, ANY, ANY],
         out_specs=VMEM,
-        scratch_shapes=[pltpu.VMEM((LIVE_DEV, width), jnp.bfloat16), pltpu.SemaphoreType.DMA],
+        scratch_shapes=[
+            pltpu.VMEM((LIVE_DEV, width), jnp.bfloat16),
+            pltpu.VMEM(panel.shape, jnp.bfloat16),
+            pltpu.SemaphoreType.DMA((5,)),
+        ],
         compiler_params=pltpu.CompilerParams(vmem_limit_bytes=24 << 20),
-        cost_estimate=pl.CostEstimate(flops=540_000_000, bytes_accessed=4_000_000, transcendentals=0),
-    )(factors, placed, panel)
+        cost_estimate=pl.CostEstimate(flops=1_350_000_000, bytes_accessed=4_000_000, transcendentals=0),
+    )(spread, where, placed, panel)
 
 
 def combine(own, incoming):
@@ -316,19 +311,15 @@
         both = both + swap(both, "yl")
         return lax.all_gather(both, "z", axis=0, tiled=True)
 
-    def fetch_panel(copies):
-        return lax.all_to_all(copies, CHIP, 0, 0, tiled=True).reshape(half, col_width)
-
     def unpack(spread, where):
         table = (where.reshape(-1, 1) == lax.iota(jnp.int32, spread.shape[0])[None, :]).astype(jnp.bfloat16)
         return dot(table, spread.astype(jnp.bfloat16), NN).astype(jnp.bfloat16)
 
-    panel = fetch_panel(copies)
+    panel = lax.all_to_all(copies, CHIP, 0, 0, tiled=True).reshape(half, col_width)
     spread = gather(keep, send)
 
-    factors = unpacked(spread, firsts)
-    incoming = swap(reduced(LIVE_DEV, factors, placed, panel), "core")
-    own = reduced(0, factors, placed, panel)
+    incoming = swap(reduced(LIVE_DEV, spread, firsts, placed, panel), "core")
+    own = reduced(0, spread, firsts, placed, panel)
     first = combine(own, incoming)
 
     def another(state):
@@ -341,8 +332,7 @@
         ]
         where = jnp.where((my_rank >= base) & (my_rank < base + CAP), my_slot - base, -1)
         factors = unpack(gather(keep, jnp.roll(send, LIVE_DEV, axis=1)), where)
-        again, _ = lax.optimization_barrier((copies, step))
-        products = remainder(dot(factors, fetch_panel(again), TN))
+        products = remainder(dot(factors, panel, TN))
         incoming = swap(products[LIVE_DEV:].astype(jnp.bfloat16), "core").astype(jnp.float32)
         result = result.astype(jnp.float32) - products[:LIVE_DEV] - incoming
         return step - 1, remainder(result).astype(jnp.int32)

time: 94.9 us -> 93.5 us (0.985)
  the two profiles are of different devices: /device:TPU:19 before, /device:TPU:3 now
where the time goes in v8:
time: 93.5 us; the launch traced here: 93.1 us
  blocking collectives  37.5 us (40%)
  starting transfers between devices  24.4 us (26%)
  waiting for transfers between devices  17.8 us (19%)
  Pallas kernels  12.4 us (13%)
    all_gather x1, blocking collectives, gather(): return lax.all_gather(both, 'z', axis=0, tiled=True)  37.5 us
    ppermute x3, waiting for transfers between devices, swap(): return lax.ppermute(value, axis, [(0, 1), (1, 0)])  17.8 us
    ppermute x3, starting transfers between devices, swap(): return lax.ppermute(value, axis, [(0, 1), (1, 0)])  17.3 us
    all_to_all x1, starting transfers between devices, shards(): lax.all_to_all(copies, CHIP, 0, 0, tiled=True).reshape(half, col_width)  7.04 us
    pallas_call x2, Pallas kernels, reduced(): pl.pallas_call(functools.partial(reduce_kernel, first_row), out_shape=jax...  5.21 us
    pallas_call x1, Pallas kernels, front(): pl.pallas_call(front_kernel, out_shape=(jax.ShapeDtypeStruct((chips, *red...  4.33 us
  transfers between devices with their start and end apart: 4, of which 2 were waited for; matrix products, arithmetic and copies ran while one was open for 0% of the time, Pallas kernels for 5%

profile of v8, /device:TPU:3, one launch (start us, length us, event | category | flops | bytes accessed | tf_op | source)
XLA Modules:
  0.0 93.1 jit_solution(18360538039678822847)
XLA Ops:
  0.0 4.3 %front.1 = (bf16[8,128,1024]{2,1,0:T(8,128)(2,1)}, bf16[512,1024]{1,0:T(8,128)(2,1)S(1)}, s16[96,512]{1,0:T(8,128)(2,1)}, s16[96,512]{1,0:T(8,128)(2,1)}, f32[2,1024]{1,0:T(2,128)S(1)}) custom-call(s32[16]{0:T(128)} %counts.1, s32[2,1024]{1,0:T(2,128)} %pivots.3, s32[512,1024]{1,0:T(8,128)} %rows.1, s32[128,1024]{1,0:T(8,128)} %bitcast.22), custom_call_target="tpu_custom_call" | custom-call | tf_op jit(solution)/shard_map/front/pallas_call | solution.py:239
  4.3 0.0 copy-start.2
  4.4 0.0 copy-start.1
  4.4 0.0 copy-start
  4.4 7.0 %all-to-all-start = ((bf16[8,128,1024]{2,1,0:T(8,128)(2,1)}), bf16[8,128,1024]{2,1,0:T(8,128)(2,1)}, u32[]{:S(2)}, u32[]{:S(2)}) async-start(bf16[8,128,1024]{2,1,0:T(8,128)(2,1)} %get-tuple-element.131), calls=%async_computation | async-start | bytes 4194304 | tf_op jit(solution)/shard_map/all_to_all | solution.py:318
  11.4 0.0 copy-done.2
  11.4 5.8 %collective-permute-start.3 = (s16[96,512]{1,0:T(8,128)(2,1)S(1)}, s16[96,512]{1,0:T(8,128)(2,1)S(1)}, u32[]{:S(2)}, u32[]{:S(2)}) collective-permute-start(s16[96,512]{1,0:T(8,128)(2,1)S(1)} %copy-done.2), channel_id=1, source_target_pairs={{0,32},{32,0},{1,33},{33,1},{2,34},{34,2},{3,35},{35,3},{4,36},{36... | collective-permute-start | bytes 294920 | tf_op jit(solution)/shard_map/ppermute | solution.py:39
  17.2 0.9 collective-permute-done.3
  18.1 0.0 copy-done.1
  18.2 1.9 %collective-permute-start.4 = (s16[96,512]{1,0:T(8,128)(2,1)S(1)}, s16[96,512]{1,0:T(8,128)(2,1)S(1)}, u32[]{:S(2)}, u32[]{:S(2)}) collective-permute-start(s16[96,512]{1,0:T(8,128)(2,1)S(1)} %add.70), channel_id=1, source_target_pairs={{0,16},{16,0},{1,17},{17,1},{2,18},{18,2},{3,19},{19,3},{4,20},{20... | collective-permute-start | bytes 294920 | tf_op jit(solution)/shard_map/ppermute | solution.py:39
  20.1 0.0 copy-done
  20.1 1.8 %ranks.1 = (s32[8,128]{1,0:T(8,128)S(1)}, s32[8,128]{1,0:T(8,128)S(1)}, s32[8,128]{1,0:T(8,128)S(1)}, s32[1]{0:T(128)}) custom-call(s32[2,1024]{1,0:T(2,128)S(1)} %copy-done), custom_call_target="tpu_custom_call" | custom-call | flops 2000000000 | bytes 1000000 | tf_op jit(solution)/shard_map/ranks/pallas_call | solution.py:260
  21.9 16.9 %collective-permute-done.4 = s16[96,512]{1,0:T(8,128)(2,1)S(1)} collective-permute-done((s16[96,512]{1,0:T(8,128)(2,1)S(1)}, s16[96,512]{1,0:T(8,128)(2,1)S(1)}, u32[]{:S(2)}, u32[]{:S(2)}) %collective-permute-start.4) | collective-permute-done | bytes 98336 | tf_op jit(solution)/shard_map/ppermute | solution.py:39
  38.8 37.5 %all-gather.2.spread = s16[1536,512]{1,0:T(8,128)(2,1)S(1)} all-gather(s16[96,512]{1,0:T(8,128)(2,1)S(1)} %add.71), channel_id=1, replica_groups=mesh['yh'=2,'x'=4,'core'=2,'yl'=2,'z'=16] {'z'}, dimensions={0}, use_global_device_ids=true | all-gather | bytes 1671168 | tf_op jit(solution)/shard_map/all_gather | solution.py:312
  76.3 0.0 all-to-all-done
  76.3 2.6 %shard_map.47 = bf16[256,1024]{1,0:T(8,128)(2,1)S(1)} custom-call(s16[1536,512]{1,0:T(8,128)(2,1)S(1)} %all-gather.2.spread, s32[8,128]{1,0:T(8,128)S(1)} %get-tuple-element.129.where, bf16[512,1024]{1,0:T(8,128)(2,1)S(1)} %get-tuple-element.210.placed, bf16[1024,1024]{1,0:T(8,128)(2,1)} %bitcast.5.panel_in), custom_call_target="tpu_custom_call" | custom-call | flops 1350000000 | bytes 4000000 | tf_op jit(solution)/shard_map/pallas_call | solution.py:273
  78.9 9.6 %collective-permute-start.5 = (bf16[256,1024]{1,0:T(8,128)(2,1)S(1)}, bf16[256,1024]{1,0:T(8,128)(2,1)S(1)}, u32[]{:S(2)}, u32[]{:S(2)}) collective-permute-start(bf16[256,1024]{1,0:T(8,128)(2,1)S(1)} %shard_map.47), channel_id=1, source_target_pairs={{0,32},{32,0},{1,33},{33,1},{2,34},{34,2},{3,35},{35,3},{4,36},{36... | collective-permute-start | bytes 1572872 | tf_op jit(solution)/shard_map/ppermute | solution.py:39
  88.5 2.6 %shard_map.46.own = bf16[256,1024]{1,0:T(8,128)(2,1)S(1)} custom-call(s16[1536,512]{1,0:T(8,128)(2,1)S(1)} %all-gather.2.spread, s32[8,128]{1,0:T(8,128)S(1)} %get-tuple-element.129.where, bf16[512,1024]{1,0:T(8,128)(2,1)S(1)} %get-tuple-element.210.placed, bf16[1024,1024]{1,0:T(8,128)(2,1)} %bitcast.5.panel_in), custom_call_target="tpu_custom_call" | custom-call | flops 1350000000 | bytes 4000000 | tf_op jit(solution)/shard_map/pallas_call | solution.py:273
  91.1 0.0 collective-permute-done.5.incoming
  91.2 1.1 %combine.1 = s32[256,1024]{1,0:T(8,128)} custom-call(bf16[256,1024]{1,0:T(8,128)(2,1)S(1)} %shard_map.46.own, bf16[256,1024]{1,0:T(8,128)(2,1)S(1)} %collective-permute-done.5.incoming), custom_call_target="tpu_custom_call" | custom-call | tf_op jit(solution)/shard_map/combine/pallas_call | solution.py:289
  92.2 0.8 while.13
  (2 shorter events, 0.1 us)
Async XLA Ops:
  4.3 7.1 %copy-start.2 = (s16[96,512]{1,0:T(8,128)(2,1)S(1)}, s16[96,512]{1,0:T(8,128)(2,1)}, u32[]{:S(2)}) copy-start(s16[96,512]{1,0:T(8,128)(2,1)} %get-tuple-element.128) | copy-start | bytes 294916
  4.4 13.8 %copy-start.1 = (s16[96,512]{1,0:T(8,128)(2,1)S(1)}, s16[96,512]{1,0:T(8,128)(2,1)}, u32[]{:S(2)}) copy-start(s16[96,512]{1,0:T(8,128)(2,1)} %get-tuple-element.127) | copy-start | bytes 294916
  4.4 15.7 %copy-start = (s32[2,1024]{1,0:T(2,128)S(1)}, s32[2,1024]{1,0:T(2,128)}, u32[]{:S(2)}) copy-start(s32[2,1024]{1,0:T(2,128)} %pivots.3) | copy-start | bytes 24580
  4.4 71.9 %all-to-all-start = ((bf16[8,128,1024]{2,1,0:T(8,128)(2,1)}), bf16[8,128,1024]{2,1,0:T(8,128)(2,1)}, u32[]{:S(2)}, u32[]{:S(2)}) async-start(bf16[8,128,1024]{2,1,0:T(8,128)(2,1)} %get-tuple-element.131), calls=%async_computation | async-start | bytes 4194304 | tf_op jit(solution)/shard_map/all_to_all | solution.py:318
  11.4 6.7 %collective-permute-start.3 = (s16[96,512]{1,0:T(8,128)(2,1)S(1)}, s16[96,512]{1,0:T(8,128)(2,1)S(1)}, u32[]{:S(2)}, u32[]{:S(2)}) collective-permute-start(s16[96,512]{1,0:T(8,128)(2,1)S(1)} %copy-done.2), channel_id=1, source_target_pairs={{0,32},{32,0},{1,33},{33,1},{2,34},{34,2},{3,35},{35,3},{4,36},{36... | collective-permute-start | bytes 294920 | tf_op jit(solution)/shard_map/ppermute | solution.py:39
  18.2 20.6 %collective-permute-start.4 = (s16[96,512]{1,0:T(8,128)(2,1)S(1)}, s16[96,512]{1,0:T(8,128)(2,1)S(1)}, u32[]{:S(2)}, u32[]{:S(2)}) collective-permute-start(s16[96,512]{1,0:T(8,128)(2,1)S(1)} %add.70), channel_id=1, source_target_pairs={{0,16},{16,0},{1,17},{17,1},{2,18},{18,2},{3,19},{19,3},{4,20},{20... | collective-permute-start | bytes 294920 | tf_op jit(solution)/shard_map/ppermute | solution.py:39
  78.9 12.3 %collective-permute-start.5 = (bf16[256,1024]{1,0:T(8,128)(2,1)S(1)}, bf16[256,1024]{1,0:T(8,128)(2,1)S(1)}, u32[]{:S(2)}, u32[]{:S(2)}) collective-permute-start(bf16[256,1024]{1,0:T(8,128)(2,1)S(1)} %shard_map.47), channel_id=1, source_target_pairs={{0,32},{32,0},{1,33},{33,1},{2,34},{34,2},{3,35},{35,3},{4,36},{36... | collective-permute-start | bytes 1572872 | tf_op jit(solution)/shard_map/ppermute | solution.py:39
